TPU v7x, 32 devices: a whole 2x2x4 slice. The times are simulated.
32 devices in a mesh: box: 4 (over y, core), dir: 8 (over z, x).
Axes of the slice: x: 2, y: 2, z: 4, core: 2. Of those that a mesh axis runs over, the one named last changes fastest.
Arguments:
- child_rad: float32 [64, 2, 128, 256], P('box', None, 'dir'), may hold values from -6 to 6
- parent_incoming: float32 [16, 2, 256, 512], P('box', None, 'dir'), may hold values from -6 to 6
- theta_interp: float32 [256, 128], replicated, may hold values from -0.5 to 0.5
- phi_interp: float32 [256, 512], replicated, may hold values from -0.375 to 0.375
- child_ops: float32 [40, 2, 128, 256], P(None, None, 'dir'), may hold values from -2 to 2
- parent_ops: float32 [40, 2, 256, 512], P(None, None, 'dir'), may hold values from -2 to 2
- child_parent: int32 [64], P('box'), may hold values from 0 to 15, as said below
- child_octant: int32 [64], P('box'), may hold values from 0 to 7, as said below
- far_child_src: int32 [64, 16], P('box'), may hold values from 0 to 63, as said below
- far_child_op: int32 [64, 16], P('box'), may hold values from 0 to 39
- far_child_len: int32 [64], P('box'), may hold values from 1 to 16
- far_parent_src: int32 [16, 8], P('box'), may hold values from 0 to 15, as said below
- far_parent_op: int32 [16, 8], P('box'), may hold values from 0 to 39
- far_parent_len: int32 [16], P('box'), may hold values from 1 to 8
Outputs:
- child_local: float32 [64, 2, 128, 256], P('box', None, 'dir')
- parent_local: float32 [16, 2, 256, 512], P('box', None, 'dir')
- parent_rad: float32 [16, 2, 256, 512], P('box', None, 'dir')
Inputs may be any that keep to these rules, and one draw needn't show every extreme that they name: child_parent never falls; the children of parents 4 q to 4 q + 3 are exactly children 16 q to 16 q + 15, every parent has 2 to 6 children. `child_octant`: children of one parent have distinct octants. far_child_src[c, k] differs from c, and far_child_src[c, k] // 16 differs from c // 16 by at most 1. far_parent_src[p, k] differs from p, and far_parent_src[p, k] // 4 differs from p // 4 by at most 1.
All inputs are finite; a program needn't handle non-finite values.
Results may differ from a plain program's by a relative error of at most 0.0003.
Values sent between devices are 32-bit elements; how exact they have to be, the bound alone decides.
A program may use at most 64 MiB of HBM per device.

v0:
```python
import functools
import math

import jax
import jax.numpy as jnp
from jax import lax
from jax.experimental import pallas as pl
from jax.experimental.pallas import tpu as pltpu
from jax.sharding import PartitionSpec as P

phase_scale = 6.0
highest = lax.Precision.HIGHEST


def neighbours(array):
    size = lax.axis_size("box")
    up = [(i, i + 1) for i in range(size - 1)]
    down = [(i + 1, i) for i in range(size - 1)]
    return lax.ppermute(array, "box", up), lax.ppermute(array, "box", down)


def octant_signs(octant):
    first = 1.0 - 2.0 * (octant % 2).astype(jnp.float32)
    second = 1.0 - 2.0 * (octant // 2 % 2).astype(jnp.float32)
    third = 1.0 - 2.0 * (octant // 4 % 2).astype(jnp.float32)
    return (first, second, third)


def phase_block(octant, row_start, row_count, total_rows, col_start, col_count, total_cols):
    angle_rows = (row_start + jnp.arange(row_count, dtype=jnp.int32)).astype(jnp.float32)
    theta = math.pi * (angle_rows + 0.5) / total_rows
    angle_cols = (col_start + jnp.arange(col_count, dtype=jnp.int32)).astype(jnp.float32)
    azimuth = 2.0 * math.pi * angle_cols / total_cols
    sin_theta = jnp.sin(theta)[:, None]
    along_x = sin_theta * jnp.cos(azimuth)[None, :]
    along_y = sin_theta * jnp.sin(azimuth)[None, :]
    along_z = jnp.cos(theta)[:, None] + 0.0 * azimuth[None, :]
    first, second, third = octant_signs(octant)
    argument = phase_scale * (
        first[:, None, None] * along_x
        + second[:, None, None] * along_y
        + third[:, None, None] * along_z
    )
    return (jnp.cos(argument), jnp.sin(argument))


def flipped(index, mask):
    result = index
    bit = 1
    while bit <= mask:
        if mask & bit:
            result = result + bit - 2 * bit * lax.rem(lax.div(index, bit), 2)
        bit *= 2
    return result


def exchange_body(count, around, fields, matrix_ref, x_ref, *refs):
    refs = list(refs)
    out_ref = refs.pop(0)
    if around:
        below_ref, above_ref = refs.pop(0), refs.pop(0)
    got, ready, landed, send_sem, recv_sem = refs[:5]
    me = lax.axis_index("dir")
    planes, depth, width = got.shape[1:]
    rows = ready.shape[2]
    mesh_ids = pl.DeviceIdType.MESH
    barrier = pltpu.get_barrier_semaphore()
    steps = range(count - 1, 0, -1)

    def partner(step):
        if count & (count - 1):
            return lax.rem(me + step, count), lax.rem(me + count - step, count)
        peer = flipped(me, step)
        return peer, peer

    for step in steps:
        pl.semaphore_signal(
            barrier, inc=1, device_id={"dir": partner(step)[0]}, device_id_type=mesh_ids
        )
    greeted = count - 1
    if around:
        box = lax.axis_index("box")
        upper = lax.rem(box + 1, fields)
        lower = lax.rem(box + fields - 1, fields)
        for other in (upper, lower):
            pl.semaphore_signal(
                barrier, inc=1, device_id={"box": other}, device_id_type=mesh_ids
            )
        greeted += 2
    pl.semaphore_wait(barrier, greeted)

    def push(source, target, leg, plane):
        for step in steps:
            peer, _ = partner(step)
            copy = pltpu.make_async_remote_copy(
                src_ref=source.at[peer, plane],
                dst_ref=target.at[me, plane],
                send_sem=send_sem.at[leg, plane, step],
                recv_sem=recv_sem.at[leg, plane, step],
                device_id={"dir": peer},
                device_id_type=mesh_ids,
            )
            copy.start()
            started.append(copy)

    def settle(target, leg, plane):
        for step in steps:
            _, origin = partner(step)
            pltpu.make_async_remote_copy(
                src_ref=target.at[origin, plane],
                dst_ref=target.at[origin, plane],
                send_sem=send_sem.at[leg, plane, step],
                recv_sem=recv_sem.at[leg, plane, step],
                device_id={"dir": origin},
                device_id_type=mesh_ids,
            ).wait_recv()

    started = []
    for plane in range(planes):
        push(x_ref, got, 0, plane)
    got[me] = x_ref[me]
    for plane in range(planes):
        settle(got, 0, plane)
        product = lax.dot_general(
            matrix_ref[...],
            got[:, plane].reshape(count * depth, width),
            (((1 if around else 0,), (0,)), ((), ())),
            precision=lax.Precision.HIGH,
            preferred_element_type=jnp.float32,
        )
        ready[:, plane] = product.reshape(count, rows, width)
        push(ready, landed, 1, plane)
    ring = []
    if around:
        box_send, box_recv = refs[5:7]
        for at, (other, target) in enumerate(((upper, below_ref), (lower, above_ref))):
            copy = pltpu.make_async_remote_copy(
                src_ref=x_ref,
                dst_ref=target,
                send_sem=box_send.at[at],
                recv_sem=box_recv.at[at],
                device_id={"box": other},
                device_id_type=mesh_ids,
            )
            copy.start()
            ring.append(copy)
    landed[me] = ready[me]
    for plane in range(planes):
        settle(landed, 1, plane)
    out_ref[...] = landed[...].reshape(out_ref.shape)
    for copy in started:
        copy.wait_send()
    for copy in ring:
        copy.wait()


def exchange(matrix, x, around, which):
    count, planes, depth, width = x.shape
    rows = matrix.shape[0 if around else 1] // count
    operands = (matrix, x)
    vmem = pl.BlockSpec(memory_space=pltpu.VMEM)
    result = jax.ShapeDtypeStruct((count * planes, rows, width), jnp.float32)
    ring = jax.ShapeDtypeStruct(x.shape, jnp.float32)
    scratch = [
        pltpu.VMEM((count, planes, depth, width), jnp.float32),
        pltpu.VMEM((count, planes, rows, width), jnp.float32),
        pltpu.VMEM((count, planes, rows, width), jnp.float32),
        pltpu.SemaphoreType.DMA((2, planes, count)),
        pltpu.SemaphoreType.DMA((2, planes, count)),
    ]
    if around:
        scratch += [pltpu.SemaphoreType.DMA((2,)), pltpu.SemaphoreType.DMA((2,))]
    return pl.pallas_call(
        functools.partial(exchange_body, count, around, lax.axis_size("box")),
        out_shape=(result, ring, ring) if around else result,
        in_specs=[vmem] * len(operands),
        out_specs=(vmem,) * 3 if around else vmem,
        scratch_shapes=scratch,
        compiler_params=pltpu.CompilerParams(
            collective_id=which, has_side_effects=True, vmem_limit_bytes=16 * 1024 * 1024
        ),
        name="exchange_" + str(which),
    )(*operands)


def translate_body(has_base, *refs):
    source_ref, which_ref, length_ref, before, own, after, ops_ref = refs[:7]
    base_ref = refs[7] if has_base else None
    out_ref, wide, sems = refs[-3:]
    boxes, _, rows, width = own.shape
    copies = [
        pltpu.make_async_copy(part, wide.at[pl.ds(at * boxes, boxes)], sems.at[at])
        for at, part in enumerate((before, own, after))
    ]
    for copy in copies:
        copy.start()
    for copy in copies:
        copy.wait()
    offset = (lax.axis_index("box") - 1) * boxes
    tall = rows
    while tall % 16 == 0 and tall * width > 4096:
        tall //= 2

    def one_box(box, carry):
        length = length_ref[box]
        for start in range(0, rows, tall):
            part = slice(start, start + tall)

            def entry(column, totals):
                real, imag = totals
                at = source_ref[box, column] - offset
                op = which_ref[box, column]
                op_real, op_imag = ops_ref[op, 0, part], ops_ref[op, 1, part]
                re, im = wide[at, 0, part], wide[at, 1, part]
                real = real + (op_real * re - op_imag * im)
                imag = imag + (op_real * im + op_imag * re)
                return real, imag

            if has_base:
                initial = (base_ref[box, 0, part], base_ref[box, 1, part])
            else:
                initial = (jnp.zeros((tall, width), jnp.float32),) * 2
            real, imag = lax.fori_loop(0, length, entry, initial)
            out_ref[box, 0, part] = real
            out_ref[box, 1, part] = imag
        return carry

    lax.fori_loop(0, boxes, one_box, 0)


def translate(own, before, after, operators, source, which_op, length, base, name):
    boxes = own.shape[0]
    vmem = pl.BlockSpec(memory_space=pltpu.VMEM)
    smem = pl.BlockSpec(memory_space=pltpu.SMEM)
    anywhere = pl.BlockSpec(memory_space=pltpu.HBM)
    operands = [source, which_op, length, before, own, after, operators]
    specs = [smem] * 3 + [anywhere] * 3 + [vmem]
    if base is not None:
        operands.append(base)
        specs.append(vmem)
    return pl.pallas_call(
        functools.partial(translate_body, base is not None),
        out_shape=jax.ShapeDtypeStruct(own.shape, jnp.float32),
        in_specs=specs,
        out_specs=vmem,
        scratch_shapes=[
            pltpu.VMEM((3 * boxes,) + own.shape[1:], jnp.float32),
            pltpu.SemaphoreType.DMA((3,)),
        ],
        compiler_params=pltpu.CompilerParams(vmem_limit_bytes=20 * 1024 * 1024),
        name=name,
    )(*operands)


def shift_body(parent_ref, octant_ref, cosine_ref, sine_ref, interp_ref, out_ref):
    children = interp_ref.shape[0]
    offset = lax.axis_index("box") * out_ref.shape[0]
    out_ref[...] = jnp.zeros_like(out_ref)

    def one_child(child, carry):
        slot, octant = parent_ref[child] - offset, octant_ref[child]
        mirrored = octant // 4
        held = octant + mirrored * (7 - 2 * octant)
        sign = (1 - 2 * mirrored).astype(jnp.float32)
        cosine, sine = cosine_ref[held], sign * sine_ref[held]
        real, imag = interp_ref[child, 0], interp_ref[child, 1]
        out_ref[slot, 0] += cosine * real - sine * imag
        out_ref[slot, 1] += sine * real + cosine * imag
        return carry

    lax.fori_loop(0, children, one_child, 0)


def unshift_body(parent_ref, octant_ref, cosine_ref, sine_ref, field_ref, out_ref):
    children = out_ref.shape[0]
    offset = lax.axis_index("box") * field_ref.shape[0]

    def one_child(child, carry):
        slot, octant = parent_ref[child] - offset, octant_ref[child]
        mirrored = octant // 4
        held = octant + mirrored * (7 - 2 * octant)
        sign = (1 - 2 * mirrored).astype(jnp.float32)
        cosine, sine = cosine_ref[held], sign * sine_ref[held]
        real, imag = field_ref[slot, 0], field_ref[slot, 1]
        out_ref[child, 0] = cosine * real + sine * imag
        out_ref[child, 1] = cosine * imag - sine * real
        return carry

    lax.fori_loop(0, children, one_child, 0)


def by_child(body, parent, octant, cosine, sine, values, boxes, name):
    vmem = pl.BlockSpec(memory_space=pltpu.VMEM)
    smem = pl.BlockSpec(memory_space=pltpu.SMEM)
    return pl.pallas_call(
        body,
        out_shape=jax.ShapeDtypeStruct((boxes,) + values.shape[1:], jnp.float32),
        in_specs=[smem] * 2 + [vmem] * 3,
        out_specs=vmem,
        compiler_params=pltpu.CompilerParams(vmem_limit_bytes=16 * 1024 * 1024),
        name=name,
    )(parent, octant, cosine, sine, values)


def per_device(
    child_rad,
    parent_incoming,
    theta_interp,
    phi_interp,
    child_ops,
    parent_ops,
    child_parent,
    child_octant,
    far_child_src,
    far_child_op,
    far_child_len,
    far_parent_src,
    far_parent_op,
    far_parent_len,
):
    child_count, _, theta_child, phi_child = child_rad.shape
    parent_count, _, theta_parent, phi_parent = parent_incoming.shape
    theta_total = theta_interp.shape[0]
    dir_count = lax.axis_size("dir")
    planes = child_count * 2 // dir_count
    padded = -(-theta_child // 8) * 8
    dir_index = lax.axis_index("dir")
    grow = ((0, 0), (0, 0), (0, padded - theta_child), (0, 0))
    spread = jnp.pad(
        theta_interp.reshape(theta_total, dir_count, theta_child),
        ((0, 0), (0, 0), (0, padded - theta_child)),
    ).reshape(theta_total, dir_count * padded)
    grown = jnp.pad(child_rad, grow)
    theta_done, before, after = exchange(
        spread, grown.reshape(dir_count, planes, padded, phi_child), True, 0
    )
    before = before.reshape(grown.shape)[:, :, :theta_child]
    after = after.reshape(grown.shape)[:, :, :theta_child]
    child_trans = translate(
        child_rad, before, after, child_ops, far_child_src, far_child_op, far_child_len, None,
        "child_translate",
    )
    theta_done = theta_done.reshape(child_count, 2, theta_parent, phi_child)
    interp = jnp.einsum("ncjf,fg->ncjg", theta_done, phi_interp, precision=lax.Precision.HIGH)
    cosine, sine = phase_block(
        jnp.arange(4, dtype=jnp.int32), dir_index * theta_parent, theta_parent, theta_total,
        0, phi_parent, phi_parent,
    )
    parent_rad = by_child(
        shift_body, child_parent, child_octant, cosine, sine, interp, parent_count, "shift"
    )
    before, after = neighbours(parent_rad)
    parent_local = translate(
        parent_rad, before, after, parent_ops, far_parent_src, far_parent_op, far_parent_len,
        parent_incoming, "parent_translate",
    )
    unshift = by_child(
        unshift_body, child_parent, child_octant, cosine, sine, parent_local, child_count, "unshift"
    )
    back_phi = jnp.einsum("ncjg,fg->ncjf", unshift, phi_interp, precision=lax.Precision.HIGH)
    anterp = exchange(
        spread, back_phi.reshape(dir_count, planes, theta_parent, phi_child), False, 1
    )
    anterp = anterp.reshape(child_count, 2, padded, phi_child)[:, :, :theta_child]
    child_local = child_trans + anterp
    return (child_local, parent_local, parent_rad)


def solution(mesh):
    in_specs = (
        P("box", None, "dir", None),
        P("box", None, "dir", None),
        P(),
        P(),
        P(None, None, "dir", None),
        P(None, None, "dir", None),
        P("box"),
        P("box"),
        P("box", None),
        P("box", None),
        P("box"),
        P("box", None),
        P("box", None),
        P("box"),
    )
    out_specs = (
        P("box", None, "dir", None),
        P("box", None, "dir", None),
        P("box", None, "dir", None),
    )
    return jax.shard_map(
        per_device, mesh=mesh, in_specs=in_specs, out_specs=out_specs, check_vma=False
    )
```

profile of v0, /device:TPU:4, one launch (start us, length us, event | category | flops | bytes accessed | tf_op | source)
XLA Modules:
  0.0 100.6 jit_solution(920456241072307555)
XLA Ops:
  0.6 0.0 copy-start
  0.8 0.1 broadcast_add_fusion
  0.9 0.0 copy-start.2
  0.9 1.0 %copy-done.2 = f32[16,2,16,256]{3,2,1,0:T(8,128)S(1)} copy-done((f32[16,2,16,256]{3,2,1,0:T(8,128)S(1)}, f32[16,2,16,256]{3,2,1,0:T(8,128)}, u32[]{:S(2)}) %copy-start.2) | copy-done | bytes 524312
  1.9 0.0 copy-start.8
  1.9 0.9 copy-done.8
  2.8 40.6 %exchange_0.1 = (f32[32,32,256]{2,1,0:T(8,128)S(1)}, f32[8,4,16,256]{3,2,1,0:T(8,128)S(1)}, f32[8,4,16,256]{3,2,1,0:T(8,128)S(1)}) custom-call(f32[256,128]{1,0:T(8,128)S(1)} %copy-done.8, f32[8,4,16,256]{3,2,1,0:T(8,128)S(1)} %bitcast.17), custom_call_target="tpu_custom_call" | custom-call | tf_op jit(solution)/shard_map/exchange_0/pallas_call | solution.py:173
  43.4 0.0 copy-done
  43.4 0.0 copy-start.14
  43.4 0.0 copy-start.15
  43.4 0.0 copy-start.6
  43.4 1.0 fusion.2.interp_ref
  44.4 0.0 copy-start.3
  44.4 0.0 copy-start.10
  44.4 0.0 copy-start.11
  44.5 0.0 copy-start.16
  44.5 0.1 broadcast_multiply_fusion.1
  44.5 1.0 %fusion.4 = (f32[4,32,512]{2,1,0:T(8,128)S(1)}, f32[4,32,512]{2,1,0:T(8,128)S(1)}) fusion(f32[32,512]{1,0:T(8,128)S(1)} %broadcast_add_fusion, f32[4]{0:T(128)S(1)} %fusion.16, f32[32,512]{1,0:T(8,128)S(1)} %get-tuple-element.12, f32[4]{0:T(128)S(1)} %get-tuple-element.18, f32[32,512]{1,0:T(8,128)S(1)} %get-tuple-element.11, f32[4]{0:T(128)S(1)} %get-tuple-element.17), kind=kLoop, calls=%fused_computation.5 | loop fusion | flops 393216 | bytes 720944 | tf_op jit(solution)/shard_map/sin | solution.py:44
  45.6 0.0 copy-done.14
  45.6 0.0 copy-done.15
  45.6 0.0 copy-start.1
  45.6 2.0 %shift.1.refs_4_ = f32[4,2,32,512]{3,2,1,0:T(8,128)} custom-call(s32[16]{0:T(128)S(1)} %copy-done.14, s32[16]{0:T(128)S(1)} %copy-done.15, f32[4,32,512]{2,1,0:T(8,128)S(1)} %get-tuple-element.10.cosine_ref, f32[4,32,512]{2,1,0:T(8,128)S(1)} %get-tuple-element.9.sine_ref, f32[16,2,32,512]{3,2,1,0:T(8,128)S(1)} %fusion.2.interp_ref), custom_call_target="tpu_custom_call" | custom-call | tf_op jit(solution)/shard_map/shift/pallas_call | solution.py:295
  47.6 0.0 copy-start.4
  47.6 0.0 copy-start.7
  47.6 0.0 copy-start.12
  47.6 0.0 copy-start.13
  47.6 0.0 copy-start.17
  47.6 2.1 %collective-permute-start.1 = (f32[4,2,32,512]{3,2,1,0:T(8,128)}, f32[4,2,32,512]{3,2,1,0:T(8,128)S(1)}, u32[]{:S(2)}, u32[]{:S(2)}) collective-permute-start(f32[4,2,32,512]{3,2,1,0:T(8,128)} %shift.1.refs_4_), channel_id=1, source_target_pairs={{8,0},{16,8},{24,16},{9,1},{17,9},{25,17},{10,2},{18,10},{26,18},{... | collective-permute-start | bytes 1572872 | tf_op jit(solution)/shard_map/ppermute | solution.py:19
  49.7 2.4 %collective-permute-start = (f32[4,2,32,512]{3,2,1,0:T(8,128)}, f32[4,2,32,512]{3,2,1,0:T(8,128)S(1)}, u32[]{:S(2)}, u32[]{:S(2)}) collective-permute-start(f32[4,2,32,512]{3,2,1,0:T(8,128)} %shift.1.refs_4_), channel_id=1, source_target_pairs={{0,8},{8,16},{16,24},{1,9},{9,17},{17,25},{2,10},{10,18},{18,26},{... | collective-permute-start | bytes 1572872 | tf_op jit(solution)/shard_map/ppermute | solution.py:19
  52.1 0.0 copy-done.6
  52.1 0.0 copy-done.3
  52.1 0.0 copy-done.10
  52.1 0.0 copy-done.11
  52.1 0.0 copy-done.16
  52.1 1.8 %child_translate.1 = f32[16,2,16,256]{3,2,1,0:T(8,128)S(1)} custom-call(s32[16,16]{1,0:T(8,128)S(1)} %copy-done.10, s32[16,16]{1,0:T(8,128)S(1)} %copy-done.11, s32[16]{0:T(128)S(1)} %copy-done.16, f32[16,2,16,256]{3,2,1,0:T(8,128)S(1)} %bitcast.19, f32[16,2,16,256]{3,2,1,0:T(8,128)S(1)} %copy-done.3, f32[16,2,16,256]{3,2,1,0:T(8,128)S(1)} %bitcast.20, ...), custom_call_target="tpu_custom_call" | custom-call | tf_op jit(solution)/shard_map/child_translate/pallas_call | solution.py:241
  53.9 2.7 %collective-permute-done.1.refs_5_ = f32[4,2,32,512]{3,2,1,0:T(8,128)S(1)} collective-permute-done((f32[4,2,32,512]{3,2,1,0:T(8,128)}, f32[4,2,32,512]{3,2,1,0:T(8,128)S(1)}, u32[]{:S(2)}, u32[]{:S(2)}) %collective-permute-start.1) | collective-permute-done | bytes 524320 | tf_op jit(solution)/shard_map/ppermute | solution.py:19
  56.6 3.7 %collective-permute-done.refs_3_ = f32[4,2,32,512]{3,2,1,0:T(8,128)S(1)} collective-permute-done((f32[4,2,32,512]{3,2,1,0:T(8,128)}, f32[4,2,32,512]{3,2,1,0:T(8,128)S(1)}, u32[]{:S(2)}, u32[]{:S(2)}) %collective-permute-start) | collective-permute-done | bytes 524320 | tf_op jit(solution)/shard_map/ppermute | solution.py:19
  60.4 0.0 copy-done.1
  60.4 0.0 copy-done.4
  60.4 0.0 copy-done.7
  60.4 0.0 copy-done.12
  60.4 0.0 copy-done.13
  60.4 0.0 copy-done.17
  60.4 1.9 %parent_translate.1.field_ref = f32[4,2,32,512]{3,2,1,0:T(8,128)} custom-call(s32[4,8]{1,0:T(4,128)S(1)} %copy-done.12, s32[4,8]{1,0:T(4,128)S(1)} %copy-done.13, s32[4]{0:T(128)S(1)} %copy-done.17, f32[4,2,32,512]{3,2,1,0:T(8,128)S(1)} %collective-permute-done.refs_3_, f32[4,2,32,512]{3,2,1,0:T(8,128)S(1)} %copy-done.4, ...), custom_call_target="tpu_custom_call" | custom-call | tf_op jit(solution)/shard_map/parent_translate/pallas_call | solution.py:241
  62.3 0.0 copy-start.5
  62.3 1.0 %copy-done.5 = f32[4,2,32,512]{3,2,1,0:T(8,128)S(1)} copy-done((f32[4,2,32,512]{3,2,1,0:T(8,128)S(1)}, f32[4,2,32,512]{3,2,1,0:T(8,128)}, u32[]{:S(2)}) %copy-start.5) | copy-done | bytes 524312
  63.3 1.1 %unshift.1 = f32[16,2,32,512]{3,2,1,0:T(8,128)S(1)} custom-call(s32[16]{0:T(128)S(1)} %copy-done.14, s32[16]{0:T(128)S(1)} %copy-done.15, f32[4,32,512]{2,1,0:T(8,128)S(1)} %get-tuple-element.10.cosine_ref, f32[4,32,512]{2,1,0:T(8,128)S(1)} %get-tuple-element.9.sine_ref, f32[4,2,32,512]{3,2,1,0:T(8,128)S(1)} %copy-done.5), custom_call_target="tpu_custom_call" | custom-call | tf_op jit(solution)/shard_map/unshift/pallas_call | solution.py:295
  64.4 0.0 copy-start.9
  64.4 1.0 %fusion = f32[16,2,32,256]{3,2,1,0:T(8,128)S(1)} fusion(f32[16,2,32,512]{3,2,1,0:T(8,128)S(1)} %unshift.1, f32[256,512]{1,0:T(8,128)S(1)} %copy-done), kind=kOutput, calls=%fused_computation | convolution fusion | flops 805306368 | bytes 3670016 | tf_op jit(solution)/shard_map/ncjg,fg->ncjf/dot_general | solution.py:360
  65.4 0.0 copy-done.9
  65.4 34.3 %exchange_1.1 = f32[32,16,256]{2,1,0:T(8,128)S(1)} custom-call(f32[256,128]{1,0:T(8,128)S(1)} %copy-done.9, f32[8,4,32,256]{3,2,1,0:T(8,128)S(1)} %bitcast.15), custom_call_target="tpu_custom_call" | custom-call | tf_op jit(solution)/shard_map/exchange_1/pallas_call | solution.py:173
  99.7 0.9 add.100
  (5 shorter events, 0.1 us)
Async XLA Ops:
  0.6 42.7 %copy-start = (f32[256,512]{1,0:T(8,128)S(1)}, f32[256,512]{1,0:T(8,128)}, u32[]{:S(2)}) copy-start(f32[256,512]{1,0:T(8,128)} %param.17) | copy-start | bytes 1572868
  0.9 1.0 %copy-start.2 = (f32[16,2,16,256]{3,2,1,0:T(8,128)S(1)}, f32[16,2,16,256]{3,2,1,0:T(8,128)}, u32[]{:S(2)}) copy-start(f32[16,2,16,256]{3,2,1,0:T(8,128)} %refs_4_.1) | copy-start | bytes 1572868
  1.9 0.9 copy-start.8
  43.4 2.2 %copy-start.14 = (s32[16]{0:T(128)S(1)}, s32[16]{0:T(128)}, u32[]{:S(2)}) copy-start(s32[16]{0:T(128)} %parent_ref.3) | copy-start | bytes 196
  43.4 2.2 %copy-start.15 = (s32[16]{0:T(128)S(1)}, s32[16]{0:T(128)}, u32[]{:S(2)}) copy-start(s32[16]{0:T(128)} %octant_ref.3) | copy-start | bytes 196
  43.4 8.7 %copy-start.6 = (f32[40,2,16,256]{3,2,1,0:T(8,128)S(1)}, f32[40,2,16,256]{3,2,1,0:T(8,128)}, u32[]{:S(2)}) copy-start(f32[40,2,16,256]{3,2,1,0:T(8,128)} %refs_6_.2) | copy-start | bytes 3932164
  44.4 7.7 %copy-start.3 = (f32[16,2,16,256]{3,2,1,0:T(8,128)S(1)}, f32[16,2,16,256]{3,2,1,0:T(8,128)}, u32[]{:S(2)}) copy-start(f32[16,2,16,256]{3,2,1,0:T(8,128)} %refs_4_.1) | copy-start | bytes 1572868
  44.4 7.7 %copy-start.10 = (s32[16,16]{1,0:T(8,128)S(1)}, s32[16,16]{1,0:T(8,128)}, u32[]{:S(2)}) copy-start(s32[16,16]{1,0:T(8,128)} %refs_0_.2) | copy-start | bytes 3076
  44.4 7.7 %copy-start.11 = (s32[16,16]{1,0:T(8,128)S(1)}, s32[16,16]{1,0:T(8,128)}, u32[]{:S(2)}) copy-start(s32[16,16]{1,0:T(8,128)} %refs_1_.2) | copy-start | bytes 3076
  44.5 7.7 %copy-start.16 = (s32[16]{0:T(128)S(1)}, s32[16]{0:T(128)}, u32[]{:S(2)}) copy-start(s32[16]{0:T(128)} %refs_2_.2) | copy-start | bytes 196
  45.6 14.8 %copy-start.1 = (f32[40,2,32,512]{3,2,1,0:T(8,128)S(1)}, f32[40,2,32,512]{3,2,1,0:T(8,128)}, u32[]{:S(2)}) copy-start(f32[40,2,32,512]{3,2,1,0:T(8,128)} %refs_6_.3) | copy-start | bytes 15728644
  47.6 12.8 %copy-start.4 = (f32[4,2,32,512]{3,2,1,0:T(8,128)S(1)}, f32[4,2,32,512]{3,2,1,0:T(8,128)}, u32[]{:S(2)}) copy-start(f32[4,2,32,512]{3,2,1,0:T(8,128)} %shift.1.refs_4_) | copy-start | bytes 1572868
  47.6 12.8 %copy-start.7 = (f32[4,2,32,512]{3,2,1,0:T(8,128)S(1)}, f32[4,2,32,512]{3,2,1,0:T(8,128)}, u32[]{:S(2)}) copy-start(f32[4,2,32,512]{3,2,1,0:T(8,128)} %refs_7_.1) | copy-start | bytes 1572868
  47.6 12.8 %copy-start.12 = (s32[4,8]{1,0:T(4,128)S(1)}, s32[4,8]{1,0:T(4,128)}, u32[]{:S(2)}) copy-start(s32[4,8]{1,0:T(4,128)} %refs_0_.3) | copy-start | bytes 388
  47.6 12.8 %copy-start.13 = (s32[4,8]{1,0:T(4,128)S(1)}, s32[4,8]{1,0:T(4,128)}, u32[]{:S(2)}) copy-start(s32[4,8]{1,0:T(4,128)} %refs_1_.3) | copy-start | bytes 388
  47.6 12.8 %copy-start.17 = (s32[4]{0:T(128)S(1)}, s32[4]{0:T(128)}, u32[]{:S(2)}) copy-start(s32[4]{0:T(128)} %refs_2_.3) | copy-start | bytes 52
  47.6 9.1 %collective-permute-start.1 = (f32[4,2,32,512]{3,2,1,0:T(8,128)}, f32[4,2,32,512]{3,2,1,0:T(8,128)S(1)}, u32[]{:S(2)}, u32[]{:S(2)}) collective-permute-start(f32[4,2,32,512]{3,2,1,0:T(8,128)} %shift.1.refs_4_), channel_id=1, source_target_pairs={{8,0},{16,8},{24,16},{9,1},{17,9},{25,17},{10,2},{18,10},{26,18},{... | collective-permute-start | bytes 1572872 | tf_op jit(solution)/shard_map/ppermute | solution.py:19
  49.7 10.7 %collective-permute-start = (f32[4,2,32,512]{3,2,1,0:T(8,128)}, f32[4,2,32,512]{3,2,1,0:T(8,128)S(1)}, u32[]{:S(2)}, u32[]{:S(2)}) collective-permute-start(f32[4,2,32,512]{3,2,1,0:T(8,128)} %shift.1.refs_4_), channel_id=1, source_target_pairs={{0,8},{8,16},{16,24},{1,9},{9,17},{17,25},{2,10},{10,18},{18,26},{... | collective-permute-start | bytes 1572872 | tf_op jit(solution)/shard_map/ppermute | solution.py:19
  62.3 1.0 %copy-start.5 = (f32[4,2,32,512]{3,2,1,0:T(8,128)S(1)}, f32[4,2,32,512]{3,2,1,0:T(8,128)}, u32[]{:S(2)}) copy-start(f32[4,2,32,512]{3,2,1,0:T(8,128)} %parent_translate.1.field_ref) | copy-start | bytes 1572868
  64.4 1.0 %copy-start.9 = (f32[256,128]{1,0:T(8,128)S(1)}, f32[256,128]{1,0:T(8,128)}, u32[]{:S(2)}) copy-start(f32[256,128]{1,0:T(8,128)} %matrix_ref.3) | copy-start | bytes 393220
where the time goes:
time: 102 us; the launch traced here: 101 us
  Pallas kernels  81.5 us (80%)
  waiting for transfers between devices  6.44 us (6%)
  starting transfers between devices  4.49 us (4%)
  local copies, waits for them, and re-layouts  3.08 us (3%)
  other arithmetic  2.18 us (2%)
  matrix products  2.01 us (2%)
    pallas_call x2, Pallas kernels, exchange(): pl.pallas_call(functools.partial(exchange_body, count, around, lax.axis_s...  74.9 us
    ppermute x2, waiting for transfers between devices, neighbours(): return (lax.ppermute(array, 'box', up), lax.ppermute(array, 'box', down))  6.44 us
    ppermute x2, starting transfers between devices, neighbours(): return (lax.ppermute(array, 'box', up), lax.ppermute(array, 'box', down))  4.49 us
    pallas_call x2, Pallas kernels, translate(): pl.pallas_call(functools.partial(translate_body, base is not None), out_s...  3.64 us
    unnamed x36, local copies, waits for them, and re-layouts  3.08 us
    pallas_call x2, Pallas kernels, by_child(): pl.pallas_call(body, out_shape=jax.ShapeDtypeStruct((boxes,) + values.sha...  3 us
  transfers between devices with their start and end apart: 2, of which 2 were waited for; matrix products, arithmetic and copies ran while one was open for 0% of the time, Pallas kernels for 2%

commit v1 on v0

--- a/solution.py
+++ b/solution.py
@@ -302,6 +302,514 @@
     )(parent, octant, cosine, sine, values)
 
 
+def within(index, size):
+    return jnp.minimum(jnp.maximum(index, 0), size - 1)
+
+
+def precise(lhs, rhs):
+    return lax.dot_general(
+        lhs,
+        rhs,
+        (((1,), (0,)), ((), ())),
+        precision=lax.Precision.HIGH,
+        preferred_element_type=jnp.float32,
+    )
+
+
+def parent_windows(children, parents, least, most):
+    windows = []
+    for p in range(parents):
+        low = max(least * p, children - most * (parents - p))
+        high = min(most * (p + 1), children - least * (parents - 1 - p))
+        windows.append((low, high))
+    return windows
+
+
+def fused_body(fields, per_chunk, *refs):
+    tables_h = refs[:8]
+    rad_h, incoming_h, theta_h, phi_h, child_ops_h, parent_ops_h = refs[8:14]
+    out_ref, local_ref, parent_rad_ref = refs[14:17]
+    (theta, phi, phi_t, theta_t, child_ops, parent_ops, near, gathered, spread, rows_in, wide,
+     cosine, sine, back, held_rows, partial, other, total, final) = refs[17:36]
+    tables = refs[36:44]
+    parent_s, octant_s, child_src_s, child_op_s, child_len_s = tables[:5]
+    parent_src_s, parent_op_s, parent_len_s = tables[5:]
+    (load_sem, half_sem, pre_send, pre_recv, in_send, in_recv, out_send, out_recv, ring_send,
+     ring_recv, parent_send, parent_recv, back_send, back_recv, raw_send, raw_recv, swap_send,
+     swap_recv, final_send, final_recv) = refs[44:]
+    mesh_ids = pl.DeviceIdType.MESH
+    me, box = lax.axis_index("dir"), lax.axis_index("box")
+    children = parent_s.shape[0]
+    parents, _, rows, width = local_ref.shape
+    depth = rad_h.shape[1]
+    half = gathered.shape[2]
+    group = 2 * per_chunk
+    chunks = children // per_chunk
+    total_rows, total_cols = theta_h.shape[0], width
+    z, x = lax.div(me, 2), lax.rem(me, 2)
+    side = lax.div(z, 2)
+    inner = z == 1 + side
+    outer = z != 1 + side
+    partner = {"dir": 2 * z + 1 - x}
+    outer_peer = [{"dir": 6 * side + at} for at in range(2)]
+    inner_peer = {"dir": 2 * (1 + side) + x}
+    across_inner = {"dir": 2 * (2 - side) + x}
+    across_outer = {"dir": 6 * (1 - side) + x}
+    has_lower, has_upper = box > 0, box < fields - 1
+    lower, upper = {"box": box - 1}, {"box": box + 1}
+
+    def remote(source, target, send, recv, device):
+        return pltpu.make_async_remote_copy(
+            src_ref=source, dst_ref=target, send_sem=send, recv_sem=recv,
+            device_id=device, device_id_type=mesh_ids,
+        )
+
+    def aligned(value, step):
+        return pl.ds(pl.multiple_of(value, step), step)
+
+    def part(k):
+        return pl.ds(k * group, group)
+
+    loads = [
+        (theta_h, theta), (phi_h, phi), (incoming_h, local_ref), (child_ops_h, child_ops),
+        (parent_ops_h, parent_ops), (rad_h, near.at[pl.ds(2 * children, 2 * children)]),
+    ]
+    loads = [
+        pltpu.make_async_copy(source, target, load_sem.at[at])
+        for at, (source, target) in enumerate(loads)
+    ]
+    table_loads = [
+        pltpu.make_async_copy(source, target, load_sem.at[6 + at])
+        for at, (source, target) in enumerate(zip(tables_h, tables))
+    ]
+    own_half = pl.ds(pl.multiple_of(x * half, half), half)
+    other_half = pl.ds(pl.multiple_of((1 - x) * half, half), half)
+    own_depth = aligned(2 * depth * z + depth * x, depth)
+    halves = [
+        pltpu.make_async_copy(
+            rad_h.at[part(k), :, own_half], gathered.at[part(k), own_depth], half_sem.at[k]
+        )
+        for k in range(chunks)
+    ]
+
+    def greet(device):
+        pl.semaphore_signal(barrier, inc=1, device_id=device, device_id_type=mesh_ids)
+
+    barrier = pltpu.get_barrier_semaphore()
+    greet(partner)
+
+    @pl.when(inner)
+    def _():
+        for device in (outer_peer[0], outer_peer[1], across_inner, across_outer):
+            greet(device)
+
+    @pl.when(outer)
+    def _():
+        for device in ({"dir": 2 * (1 + side)}, {"dir": 2 * (1 + side) + 1}, across_inner):
+            greet(device)
+
+    pl.when(has_lower)(lambda: greet(lower))
+    pl.when(has_upper)(lambda: greet(upper))
+    for copy in halves:
+        copy.start()
+    for copy in table_loads + loads:
+        copy.start()
+    pl.semaphore_wait(
+        barrier,
+        4 + inner.astype(jnp.int32) + has_lower.astype(jnp.int32) + has_upper.astype(jnp.int32),
+    )
+
+    sent, sent_inner, sent_outer = [], [], []
+
+    def launch(record, build):
+        record.append(build)
+        remote(*build()).start()
+
+    def landed(target, send, recv):
+        remote(target, target, send, recv, partner).wait_recv()
+
+    for k in range(chunks):
+        launch(sent, lambda k=k: (rad_h.at[part(k), :, other_half], gathered.at[part(k), own_depth], pre_send.at[k], pre_recv.at[k], partner))
+    rings = ((has_upper, upper, 0), (has_lower, lower, 4 * children))
+    for at, (exists, device, start) in enumerate(rings):
+        @pl.when(exists)
+        def _():
+            remote(
+                rad_h, near.at[pl.ds(start, 2 * children)], ring_send.at[at], ring_recv.at[at], device
+            ).start()
+
+    partner_depth = aligned(2 * depth * z + depth * (1 - x), depth)
+    own_block = aligned(2 * depth * z, 2 * depth)
+
+    def forward(k):
+        halves[k].wait()
+        landed(gathered.at[part(k), partner_depth], pre_send.at[k], pre_recv.at[k])
+        block = gathered.at[part(k), own_block]
+
+        @pl.when(inner)
+        def _():
+            launch(sent_inner, lambda k=k: (block, block, in_send.at[0, k], in_recv.at[1, k], across_inner))
+
+        @pl.when(outer)
+        def _():
+            launch(sent_outer, lambda k=k: (block, block, in_send.at[0, k], in_recv.at[0, k], inner_peer))
+            launch(sent_outer, lambda k=k: (block, block, in_send.at[1, k], in_recv.at[2, k], across_inner))
+
+    for k in range(chunks):
+        forward(k)
+
+    row_at = lax.broadcasted_iota(jnp.int32, (rows, width), 0) + me * rows
+    col_at = lax.broadcasted_iota(jnp.int32, (rows, width), 1)
+    polar = math.pi * (row_at.astype(jnp.float32) + 0.5) / total_rows
+    azimuth = 2.0 * math.pi * col_at.astype(jnp.float32) / total_cols
+    sin_polar = jnp.sin(polar)
+    along_x = sin_polar * jnp.cos(azimuth)
+    along_y = sin_polar * jnp.sin(azimuth)
+    along_z = jnp.cos(polar)
+    for octant in range(4):
+        first, second = 1.0 - 2.0 * (octant % 2), 1.0 - 2.0 * (octant // 2)
+        argument = phase_scale * (first * along_x + second * along_y + along_z)
+        cosine[octant] = jnp.cos(argument)
+        sine[octant] = jnp.sin(argument)
+    for copy in table_loads:
+        copy.wait()
+    loads[0].wait()
+    loads[1].wait()
+    side_rows = aligned(total_rows // 2 * side, total_rows // 2)
+    phi_t[...] = phi[...].T
+    theta_t[...] = theta[side_rows].T
+
+    def phases(child):
+        octant = octant_s[child]
+        mirrored = octant // 4
+        held = octant + mirrored * (7 - 2 * octant)
+        return held, (1 - 2 * mirrored).astype(jnp.float32)
+
+    def theta_stage(k):
+        own, near_z, far_z = 2 * depth * 3 * side, 2 * depth * (2 - side), 2 * depth * 3 * (1 - side)
+        for at, start in enumerate((own, near_z, far_z)):
+            landed(gathered.at[part(k), aligned(start, 2 * depth)], in_send.at[0, k], in_recv.at[at, k])
+        block = jnp.concatenate([gathered[k * group + j] for j in range(group)], axis=1)
+        product = precise(theta[side_rows], block)
+        for j in range(group):
+            spread[k * group + j] = product[:, j * half : (j + 1) * half]
+        rows_in[x, part(k)] = spread[part(k), aligned(2 * rows * (1 - side) + rows * x, rows)]
+        launch(sent_inner, lambda k=k: (spread.at[part(k), aligned(2 * rows * (1 - side) + rows * (1 - x), rows)], rows_in.at[x, part(k)], out_send.at[0, k], out_recv.at[x, k], partner))
+        for at in range(2):
+            launch(sent_inner, lambda k=k, at=at: (spread.at[part(k), aligned(2 * rows * side + rows * at, rows)], rows_in.at[x, part(k)], out_send.at[1 + at, k], out_recv.at[x, k], outer_peer[at]))
+
+    windows = parent_windows(children, parents, 2, 6)
+
+    def shift_stage(k):
+        @pl.when(inner)
+        def _():
+            landed(rows_in.at[1 - x, part(k)], out_send.at[0, k], out_recv.at[1 - x, k])
+
+        @pl.when(outer)
+        def _():
+            for at in range(2):
+                landed(rows_in.at[at, part(k)], out_send.at[0, k], out_recv.at[at, k])
+
+        block = jnp.concatenate(
+            [rows_in[at, part(k)].reshape(group * rows, half) for at in range(2)], axis=1
+        )
+        product = precise(block, phi[...])
+        for i in range(per_chunk):
+            child = k * per_chunk + i
+            held, sign = phases(child)
+            slot = parent_s[child] - box * parents
+            for t in range(0, rows, 8):
+                tile = slice(t, t + 8)
+                real = product[2 * i * rows + t : 2 * i * rows + t + 8]
+                imag = product[(2 * i + 1) * rows + t : (2 * i + 1) * rows + t + 8]
+                cos, sin = cosine[held, tile], sign * sine[held, tile]
+                moved = (cos * real - sin * imag, sin * real + cos * imag)
+                for p, (low, high) in enumerate(windows):
+                    if not low <= child < high:
+                        continue
+                    belongs = (slot == p).astype(jnp.float32)
+                    for plane in range(2):
+                        term = belongs * moved[plane]
+                        if child == low:
+                            wide[parents + p, plane, tile] = term
+                        else:
+                            wide[parents + p, plane, tile] += term
+        for p, (low, high) in enumerate(windows):
+            if k * per_chunk < high <= (k + 1) * per_chunk:
+                for at, (exists, device) in enumerate(((has_upper, upper), (has_lower, lower))):
+                    @pl.when(exists)
+                    def _():
+                        remote(
+                            wide.at[parents + p], wide.at[2 * parents * at + p],
+                            parent_send.at[at, p], parent_recv.at[at, p], device,
+                        ).start()
+
+    for step in range(chunks + 1):
+        if step < chunks:
+            pl.when(inner)(functools.partial(theta_stage, step))
+        if step >= 1:
+            shift_stage(step - 1)
+
+    loads[2].wait()
+    loads[4].wait()
+    for at, exists in enumerate((has_lower, has_upper)):
+        @pl.when(exists)
+        def _():
+            for p in range(parents):
+                landed(wide.at[2 * parents * at + p], parent_send.at[at, p], parent_recv.at[at, p])
+
+    tiles = rows // 8
+
+    def translate_tile(step, carry):
+        p, t = lax.div(step, tiles), lax.rem(step, tiles)
+        tile = pl.ds(pl.multiple_of(t * 8, 8), 8)
+        real, imag = local_ref[p, 0, tile], local_ref[p, 1, tile]
+        length = parent_len_s[p]
+        for column in range(parent_src_s.shape[1]):
+            at = within(parent_src_s[p, column] - (box - 1) * parents, 3 * parents)
+            op = parent_op_s[p, column]
+            live = (column < length).astype(jnp.float32)
+            op_real, op_imag = live * parent_ops[op, 0, tile], live * parent_ops[op, 1, tile]
+            re, im = wide[at, 0, tile], wide[at, 1, tile]
+            real = real + (op_real * re - op_imag * im)
+            imag = imag + (op_real * im + op_imag * re)
+        local_ref[p, 0, tile] = real
+        local_ref[p, 1, tile] = imag
+        return carry
+
+    lax.fori_loop(0, parents * tiles, translate_tile, 0)
+
+    z_local = z - 2 * side
+    own_rows = aligned(2 * rows * z_local + rows * x, rows)
+    partner_rows = aligned(2 * rows * z_local + rows * (1 - x), rows)
+
+    def unshift_stage(k):
+        fields_in = []
+        for i in range(per_chunk):
+            child = k * per_chunk + i
+            held, sign = phases(child)
+            slot = within(parent_s[child] - box * parents, parents)
+            cos, sin = cosine[held], sign * sine[held]
+            real, imag = local_ref[slot, 0], local_ref[slot, 1]
+            fields_in += [cos * real + sin * imag, cos * imag - sin * real]
+        product = precise(jnp.concatenate(fields_in, axis=0), phi_t[...])
+        for at in range(2):
+            back[at, part(k)] = product[:, at * half : (at + 1) * half].reshape(group, rows, half)
+        held_rows[part(k), own_rows] = back[x, part(k)]
+        launch(sent, lambda k=k: (back.at[1 - x, part(k)], held_rows.at[part(k), own_rows], back_send.at[k], back_recv.at[k], partner))
+
+    def raise_stage(k):
+        landed(held_rows.at[part(k), partner_rows], back_send.at[k], back_recv.at[k])
+        launch(sent_outer, lambda k=k: (
+            held_rows.at[part(k), aligned(2 * rows * side, 2 * rows)],
+            held_rows.at[part(k), aligned(2 * rows * side, 2 * rows)],
+            raw_send.at[k], raw_recv.at[k], inner_peer,
+        ))
+
+    def gather_stage(k):
+        landed(held_rows.at[part(k), partner_rows], back_send.at[k], back_recv.at[k])
+        landed(
+            held_rows.at[part(k), aligned(2 * rows * side, 2 * rows)], raw_send.at[k], raw_recv.at[k]
+        )
+        block = jnp.concatenate([held_rows[k * group + j] for j in range(group)], axis=1)
+        product = precise(theta_t[...], block)
+        for j in range(group):
+            partial[k * group + j] = product[:, j * half : (j + 1) * half]
+        launch(sent_inner, lambda k=k: (partial.at[part(k), aligned(4 * depth * (1 - side), 4 * depth)], other.at[part(k)], swap_send.at[k], swap_recv.at[k], across_inner))
+
+    def combine_stage(k):
+        landed(other.at[part(k)], swap_send.at[k], swap_recv.at[k])
+        total[part(k)] = partial[part(k), aligned(4 * depth * side, 4 * depth)] + other[part(k)]
+        final[x, part(k)] = total[part(k), aligned(2 * depth * (1 - side) + depth * x, depth)]
+        launch(sent_inner, lambda k=k: (total.at[part(k), aligned(2 * depth * (1 - side) + depth * (1 - x), depth)], final.at[x, part(k)], final_send.at[0, k], final_recv.at[x, k], partner))
+        for at in range(2):
+            launch(sent_inner, lambda k=k, at=at: (total.at[part(k), aligned(2 * depth * side + depth * at, depth)], final.at[x, part(k)], final_send.at[1 + at, k], final_recv.at[x, k], outer_peer[at]))
+
+    def child_translate(child, carry):
+        real = jnp.zeros((depth, out_ref.shape[2]), jnp.float32)
+        imag = real
+        length = child_len_s[child]
+        for column in range(child_src_s.shape[1]):
+            at = 2 * within(child_src_s[child, column] - (box - 1) * children, 3 * children)
+            op = child_op_s[child, column]
+            live = (column < length).astype(jnp.float32)
+            op_real, op_imag = live * child_ops[op, 0], live * child_ops[op, 1]
+            re, im = near[at], near[at + 1]
+            real = real + (op_real * re - op_imag * im)
+            imag = imag + (op_real * im + op_imag * re)
+        out_ref[2 * child] = real
+        out_ref[2 * child + 1] = imag
+        return carry
+
+    def finish_stage(k):
+        @pl.when(inner)
+        def _():
+            landed(final.at[1 - x, part(k)], final_send.at[0, k], final_recv.at[1 - x, k])
+
+        @pl.when(outer)
+        def _():
+            for at in range(2):
+                landed(final.at[at, part(k)], final_send.at[0, k], final_recv.at[at, k])
+
+        for at in range(2):
+            columns = slice(at * half, (at + 1) * half)
+            out_ref[part(k), :, columns] += final[at, part(k)]
+
+    lag = 2
+    for step in range(chunks + lag + 1):
+        if step < chunks:
+            unshift_stage(step)
+        if 1 <= step <= chunks:
+            pl.when(outer)(functools.partial(raise_stage, step - 1))
+        if step == lag:
+            loads[3].wait()
+            loads[5].wait()
+            for at, (exists, start) in enumerate(((has_lower, 0), (has_upper, 4 * children))):
+                @pl.when(exists)
+                def _():
+                    landed(near.at[pl.ds(start, 2 * children)], ring_send.at[at], ring_recv.at[at])
+            parent_rad_ref[...] = wide[parents : 2 * parents]
+        if lag <= step < chunks + lag:
+            first = (step - lag) * per_chunk
+            lax.fori_loop(first, first + per_chunk, child_translate, 0)
+            pl.when(inner)(functools.partial(gather_stage, step - lag))
+        if lag + 1 <= step:
+            pl.when(inner)(functools.partial(combine_stage, step - lag - 1))
+    for k in range(chunks):
+        finish_stage(k)
+
+    for build in sent:
+        remote(*build()).wait_send()
+
+    @pl.when(inner)
+    def _():
+        for build in sent_inner:
+            remote(*build()).wait_send()
+
+    @pl.when(outer)
+    def _():
+        for build in sent_outer:
+            remote(*build()).wait_send()
+
+    for at, (exists, device, start) in enumerate(rings):
+        @pl.when(exists)
+        def _():
+            remote(
+                rad_h, near.at[pl.ds(start, 2 * children)], ring_send.at[at], ring_recv.at[at], device
+            ).wait_send()
+            for p in range(parents):
+                remote(
+                    wide.at[parents + p], wide.at[2 * parents * at + p],
+                    parent_send.at[at, p], parent_recv.at[at, p], device,
+                ).wait_send()
+
+
+def deliver_body(*refs):
+    sems = refs[-1]
+    count = (len(refs) - 1) // 2
+    copies = [
+        pltpu.make_async_copy(refs[at], refs[count + at], sems.at[at]) for at in range(count)
+    ]
+    for copy in copies:
+        copy.start()
+    for copy in copies:
+        copy.wait()
+
+
+def deliver(*arrays):
+    return pl.pallas_call(
+        deliver_body,
+        out_shape=tuple(jax.ShapeDtypeStruct(array.shape, array.dtype) for array in arrays),
+        in_specs=[pl.BlockSpec(memory_space=pltpu.VMEM)] * len(arrays),
+        out_specs=(pl.BlockSpec(memory_space=pltpu.HBM),) * len(arrays),
+        scratch_shapes=[pltpu.SemaphoreType.DMA((len(arrays),))],
+        compiler_params=pltpu.CompilerParams(vmem_limit_bytes=1024 * 1024),
+        name="deliver",
+    )(*arrays)
+
+
+def fused(
+    child_rad, parent_incoming, theta_interp, phi_interp, child_ops, parent_ops, *tables
+):
+    children, _, depth, phi_child = child_rad.shape
+    parents, _, rows, width = parent_incoming.shape
+    total_rows, total_depth = theta_interp.shape
+    per_chunk = 2
+    chunks = children // per_chunk
+    half = phi_child // 2
+    planes = 2 * children
+    vmem = pl.BlockSpec(memory_space=pltpu.VMEM)
+    hbm = pl.BlockSpec(memory_space=pltpu.HBM)
+
+    def room(*shape):
+        return pltpu.VMEM(shape, jnp.float32)
+
+    dma = pltpu.SemaphoreType.DMA
+    scratch = [
+        room(total_rows, total_depth),
+        room(phi_child, width),
+        room(width, phi_child),
+        room(total_depth, total_rows // 2),
+        room(*child_ops.shape),
+        room(*parent_ops.shape),
+        room(3 * planes, depth, phi_child),
+        room(planes, total_depth, half),
+        room(planes, total_rows // 2, half),
+        room(2, planes, rows, half),
+        room(3 * parents, 2, rows, width),
+        room(4, rows, width),
+        room(4, rows, width),
+        room(2, planes, rows, half),
+        room(planes, total_rows // 2, half),
+        room(planes, total_depth, half),
+        room(planes, total_depth // 2, half),
+        room(planes, total_depth // 2, half),
+        room(2, planes, depth, half),
+        *(pltpu.SMEM(table.shape, jnp.int32) for table in tables),
+        dma((14,)),
+        dma((chunks,)),
+        dma((chunks,)),
+        dma((chunks,)),
+        dma((2, chunks)),
+        dma((3, chunks)),
+        dma((3, chunks)),
+        dma((2, chunks)),
+        dma((2,)),
+        dma((2,)),
+        dma((2, parents)),
+        dma((2, parents)),
+        dma((chunks,)),
+        dma((chunks,)),
+        dma((chunks,)),
+        dma((chunks,)),
+        dma((chunks,)),
+        dma((chunks,)),
+        dma((3, chunks)),
+        dma((2, chunks)),
+    ]
+    operands = (
+        *tables, child_rad.reshape(planes, depth, phi_child), parent_incoming, theta_interp,
+        phi_interp, child_ops, parent_ops,
+    )
+    anterp, local, rad = pl.pallas_call(
+        functools.partial(fused_body, lax.axis_size("box"), per_chunk),
+        out_shape=(
+            jax.ShapeDtypeStruct((planes, depth, phi_child), jnp.float32),
+            jax.ShapeDtypeStruct(parent_incoming.shape, jnp.float32),
+            jax.ShapeDtypeStruct(parent_incoming.shape, jnp.float32),
+        ),
+        in_specs=[hbm] * len(operands),
+        out_specs=(vmem,) * 3,
+        scratch_shapes=scratch,
+        compiler_params=pltpu.CompilerParams(
+            collective_id=0, has_side_effects=True, vmem_limit_bytes=40 * 1024 * 1024
+        ),
+        name="level_pass",
+    )(*(pltpu.with_memory_space_constraint(operand, pltpu.HBM) for operand in operands))
+    anterp, local, rad = deliver(anterp, local, rad)
+    return anterp.reshape(child_rad.shape), local, rad
+
+
 def per_device(
     child_rad,
     parent_incoming,
@@ -322,6 +830,12 @@
     parent_count, _, theta_parent, phi_parent = parent_incoming.shape
     theta_total = theta_interp.shape[0]
     dir_count = lax.axis_size("dir")
+    if dir_count == 8 and theta_child % 8 == 0 and phi_child % 256 == 0 and child_count % 2 == 0:
+        return fused(
+            child_rad, parent_incoming, theta_interp, phi_interp, child_ops, parent_ops, child_parent,
+            child_octant, far_child_src, far_child_op, far_child_len, far_parent_src, far_parent_op,
+            far_parent_len,
+        )
     planes = child_count * 2 // dir_count
     padded = -(-theta_child // 8) * 8
     dir_index = lax.axis_index("dir")

time: 102 us -> 80.3 us (0.79)
  waiting for transfers between devices: 6.44 us -> 0 us
  starting transfers between devices: 4.49 us -> 0 us
  local copies, waits for them, and re-layouts: 3.08 us -> 0 us
  Pallas kernels: 81.5 us -> 79.2 us
  other arithmetic: 2.18 us -> 0 us
  matrix products: 2.01 us -> 0 us
    ppermute x2 -> x0, waiting for transfers between devices: 6.44 us -> none  [neighbours(): return (lax.ppermute(array, 'box', up), lax.ppermute(array, 'box', down))]
    ppermute x2 -> x0, starting transfers between devices: 4.49 us -> none  [neighbours(): return (lax.ppermute(array, 'box', up), lax.ppermute(array, 'box', down))]
    unnamed x36 -> x0, local copies, waits for them, and re-layouts: 3.08 us -> none
    pallas_call x6 -> x2, Pallas kernels: 81.5 us -> 79.2 us  [the longest x1 78 us: fused(): pl.pallas_call(functools.partial(fused_body, lax.axis_size('box'), per_ch...]
    dot_general x2 -> x0, matrix products: 2.01 us -> none  [the longest x1 1.02 us: per_device(): jnp.einsum('ncjg,fg->ncjf', unshift, phi_interp, precision=lax.Precision....]
    sin x2 -> x0, other arithmetic: 1.08 us -> none  [the longest x1 1.03 us: phase_block(): return (jnp.cos(argument), jnp.sin(argument))]
  transfers between devices with their start and end apart: 2 -> 0, of which waited for: 2 -> 0; matrix products, arithmetic and copies ran while one was open for 0% -> 0% of each run, Pallas kernels for 2% -> 0%
where the time goes in v1:
time: 80.3 us; the launch traced here: 79.8 us
  Pallas kernels  79.2 us (99%)
    pallas_call x1, Pallas kernels, fused(): pl.pallas_call(functools.partial(fused_body, lax.axis_size('box'), per_ch...  78 us

profile of v1, /device:TPU:4, one launch (start us, length us, event | category | flops | bytes accessed | tf_op | source)
XLA Modules:
  0.0 79.8 jit_solution(12806062246201646767)
XLA Ops:
  0.6 78.0 %level_pass.1 = (f32[32,16,256]{2,1,0:T(8,128)S(1)}, f32[4,2,32,512]{3,2,1,0:T(8,128)S(1)}, f32[4,2,32,512]{3,2,1,0:T(8,128)S(1)}) custom-call(s32[16]{0:T(128)} %refs_0_.1, s32[16]{0:T(128)} %refs_1_.1, s32[16,16]{1,0:T(8,128)} %refs_2_.1, s32[16,16]{1,0:T(8,128)} %refs_3_.1, s32[16]{0:T(128)} %refs_4_.1, s32[4,8]{1,0:T(4,128)} %refs_5_.1, s32[4,8]{1,0:T(4,128)} %refs_6_.1, ...), custom_call_target="tpu_custom_call" | custom-call | tf_op jit(solution)/shard_map/level_pass/pallas_call | solution.py:794
  78.7 1.2 %deliver.1 = (f32[32,16,256]{2,1,0:T(8,128)}, f32[4,2,32,512]{3,2,1,0:T(8,128)}, f32[4,2,32,512]{3,2,1,0:T(8,128)}) custom-call(f32[32,16,256]{2,1,0:T(8,128)S(1)} %get-tuple-element.9.refs_0_, f32[4,2,32,512]{3,2,1,0:T(8,128)S(1)} %get-tuple-element.10.refs_1_, f32[4,2,32,512]{3,2,1,0:T(8,128)S(1)} %get-tuple-element.11.refs_2_), custom_call_target="tpu_custom_call" | custom-call | tf_op jit(solution)/shard_map/deliver/pallas_call | solution.py:720

commit v2 on v1

--- a/solution.py
+++ b/solution.py
@@ -325,7 +325,7 @@
     return windows
 
 
-def fused_body(fields, per_chunk, *refs):
+def fused_body(fields, sizes, *refs):
     tables_h = refs[:8]
     rad_h, incoming_h, theta_h, phi_h, child_ops_h, parent_ops_h = refs[8:14]
     out_ref, local_ref, parent_rad_ref = refs[14:17]
@@ -334,7 +334,7 @@
     tables = refs[36:44]
     parent_s, octant_s, child_src_s, child_op_s, child_len_s = tables[:5]
     parent_src_s, parent_op_s, parent_len_s = tables[5:]
-    (load_sem, half_sem, pre_send, pre_recv, in_send, in_recv, out_send, out_recv, ring_send,
+    (load_sem, pre_send, pre_recv, in_send, in_recv, out_send, out_recv, ring_send,
      ring_recv, parent_send, parent_recv, back_send, back_recv, raw_send, raw_recv, swap_send,
      swap_recv, final_send, final_recv) = refs[44:]
     mesh_ids = pl.DeviceIdType.MESH
@@ -343,20 +343,28 @@
     parents, _, rows, width = local_ref.shape
     depth = rad_h.shape[1]
     half = gathered.shape[2]
-    group = 2 * per_chunk
-    chunks = children // per_chunk
+    chunks, direct, early = len(sizes), 2, 2
+    starts = [sum(sizes[:k]) for k in range(chunks)]
     total_rows, total_cols = theta_h.shape[0], width
     z, x = lax.div(me, 2), lax.rem(me, 2)
     side = lax.div(z, 2)
     inner = z == 1 + side
     outer = z != 1 + side
-    partner = {"dir": 2 * z + 1 - x}
-    outer_peer = [{"dir": 6 * side + at} for at in range(2)]
-    inner_peer = {"dir": 2 * (1 + side) + x}
-    across_inner = {"dir": 2 * (2 - side) + x}
-    across_outer = {"dir": 6 * (1 - side) + x}
+
+    def at_place(place):
+        return {"box": box, "dir": place}
+
+    partner = at_place(2 * z + 1 - x)
+    outer_peer = [at_place(6 * side + at) for at in range(2)]
+    inner_peers = [at_place(2 * (1 + side) + at) for at in range(2)]
+    inner_peer = at_place(2 * (1 + side) + x)
+    across_inner = at_place(2 * (2 - side) + x)
+    across_inners = [at_place(2 * (2 - side) + at) for at in range(2)]
+    across_outers = [at_place(6 * (1 - side) + at) for at in range(2)]
+    inner_diagonal = at_place(2 * (1 + side) + 1 - x)
+    across_diagonal = at_place(2 * (2 - side) + 1 - x)
     has_lower, has_upper = box > 0, box < fields - 1
-    lower, upper = {"box": box - 1}, {"box": box + 1}
+    lower, upper = {"box": box - 1, "dir": me}, {"box": box + 1, "dir": me}
 
     def remote(source, target, send, recv, device):
         return pltpu.make_async_remote_copy(
@@ -368,16 +376,17 @@
         return pl.ds(pl.multiple_of(value, step), step)
 
     def part(k):
-        return pl.ds(k * group, group)
-
+        return pl.ds(2 * starts[k], 2 * sizes[k])
+
+    own_near = pl.ds(2 * children, 2 * children)
     loads = [
-        (theta_h, theta), (phi_h, phi), (incoming_h, local_ref), (child_ops_h, child_ops),
-        (parent_ops_h, parent_ops), (rad_h, near.at[pl.ds(2 * children, 2 * children)]),
+        (rad_h, near.at[own_near]), (theta_h, theta), (phi_h, phi), (incoming_h, local_ref),
+        (child_ops_h, child_ops), (parent_ops_h, parent_ops),
     ]
-    loads = [
+    near_load, theta_load, phi_load, incoming_load, child_load, parent_load = (
         pltpu.make_async_copy(source, target, load_sem.at[at])
         for at, (source, target) in enumerate(loads)
-    ]
+    )
     table_loads = [
         pltpu.make_async_copy(source, target, load_sem.at[6 + at])
         for at, (source, target) in enumerate(zip(tables_h, tables))
@@ -385,12 +394,20 @@
     own_half = pl.ds(pl.multiple_of(x * half, half), half)
     other_half = pl.ds(pl.multiple_of((1 - x) * half, half), half)
     own_depth = aligned(2 * depth * z + depth * x, depth)
-    halves = [
-        pltpu.make_async_copy(
-            rad_h.at[part(k), :, own_half], gathered.at[part(k), own_depth], half_sem.at[k]
-        )
-        for k in range(chunks)
-    ]
+    def fill_phases():
+        row_at = lax.broadcasted_iota(jnp.int32, (rows, width), 0) + me * rows
+        col_at = lax.broadcasted_iota(jnp.int32, (rows, width), 1)
+        polar = math.pi * (row_at.astype(jnp.float32) + 0.5) / total_rows
+        azimuth = 2.0 * math.pi * col_at.astype(jnp.float32) / total_cols
+        sin_polar = jnp.sin(polar)
+        along_x = sin_polar * jnp.cos(azimuth)
+        along_y = sin_polar * jnp.sin(azimuth)
+        along_z = jnp.cos(polar)
+        for octant in range(4):
+            first, second = 1.0 - 2.0 * (octant % 2), 1.0 - 2.0 * (octant // 2)
+            argument = phase_scale * (first * along_x + second * along_y + along_z)
+            cosine[octant] = jnp.cos(argument)
+            sine[octant] = jnp.sin(argument)
 
     def greet(device):
         pl.semaphore_signal(barrier, inc=1, device_id=device, device_id_type=mesh_ids)
@@ -400,193 +417,251 @@
 
     @pl.when(inner)
     def _():
-        for device in (outer_peer[0], outer_peer[1], across_inner, across_outer):
+        for device in outer_peer + across_inners + across_outers:
             greet(device)
 
     @pl.when(outer)
     def _():
-        for device in ({"dir": 2 * (1 + side)}, {"dir": 2 * (1 + side) + 1}, across_inner):
+        for device in inner_peers + across_inners:
             greet(device)
 
     pl.when(has_lower)(lambda: greet(lower))
     pl.when(has_upper)(lambda: greet(upper))
-    for copy in halves:
+    for copy in (near_load, *table_loads, theta_load, phi_load):
         copy.start()
-    for copy in table_loads + loads:
-        copy.start()
+    fill_phases()
+    near_load.wait()
     pl.semaphore_wait(
         barrier,
-        4 + inner.astype(jnp.int32) + has_lower.astype(jnp.int32) + has_upper.astype(jnp.int32),
-    )
-
-    sent, sent_inner, sent_outer = [], [], []
-
-    def launch(record, build):
-        record.append(build)
-        remote(*build()).start()
+        5 + 2 * inner.astype(jnp.int32) + has_lower.astype(jnp.int32) + has_upper.astype(jnp.int32),
+    )
 
     def landed(target, send, recv):
         remote(target, target, send, recv, partner).wait_recv()
 
-    for k in range(chunks):
-        launch(sent, lambda k=k: (rad_h.at[part(k), :, other_half], gathered.at[part(k), own_depth], pre_send.at[k], pre_recv.at[k], partner))
+    def each(first, count, body):
+        for k in range(first, count):
+            body(k)
+
+    partner_depth = aligned(2 * depth * z + depth * (1 - x), depth)
+
+    def mine(k, columns):
+        return near.at[pl.ds(2 * (children + starts[k]), 2 * sizes[k]), :, columns]
+
+    def trade(k):
+        return remote(
+            mine(k, other_half), gathered.at[part(k), own_depth], pre_send.at[0], pre_recv.at[k],
+            partner,
+        )
+
+    def supply(k, relayed, devices):
+        target = gathered.at[part(k), own_depth]
+        source, device = mine(k, own_half), devices[0]
+        if relayed and k < direct:
+            source, device = mine(k, other_half), devices[1]
+        elif relayed:
+            source = target = gathered.at[part(k), partner_depth]
+        return remote(source, target, in_send.at[0], in_recv.at[k], device)
+
+    def inner_supply(k, relayed):
+        return [supply(k, relayed, (across_inner, across_diagonal))]
+
+    def outer_supply(k, relayed):
+        return [
+            supply(k, relayed, (inner_peer, inner_diagonal)),
+            supply(k, relayed, (across_inner, across_diagonal)),
+        ]
+
+    def start(copies):
+        for copy in copies:
+            copy.start()
+
+    def traded(k):
+        landed(gathered.at[part(k), partner_depth], pre_send.at[0], pre_recv.at[k])
+
+    def advance(k, copies):
+        traded(k)
+        start(copies(k, 1))
+        if k + early < chunks:
+            trade(k + early).start()
+            start(copies(k + early, 0))
+
+    def open_supply(copies):
+        for k in range(direct):
+            start(copies(k, 0))
+            start(copies(k, 1))
+        for k in range(direct, direct + early):
+            start(copies(k, 0))
+
+    pl.when(inner)(lambda: start([trade(k) for k in range(direct)]))
+    start([trade(k) for k in range(direct, direct + early)])
+    pl.when(inner)(lambda: open_supply(inner_supply))
+    pl.when(outer)(lambda: open_supply(outer_supply))
     rings = ((has_upper, upper, 0), (has_lower, lower, 4 * children))
-    for at, (exists, device, start) in enumerate(rings):
-        @pl.when(exists)
-        def _():
-            remote(
-                rad_h, near.at[pl.ds(start, 2 * children)], ring_send.at[at], ring_recv.at[at], device
-            ).start()
-
-    partner_depth = aligned(2 * depth * z + depth * (1 - x), depth)
-    own_block = aligned(2 * depth * z, 2 * depth)
-
-    def forward(k):
-        halves[k].wait()
-        landed(gathered.at[part(k), partner_depth], pre_send.at[k], pre_recv.at[k])
-        block = gathered.at[part(k), own_block]
-
-        @pl.when(inner)
-        def _():
-            launch(sent_inner, lambda k=k: (block, block, in_send.at[0, k], in_recv.at[1, k], across_inner))
-
-        @pl.when(outer)
-        def _():
-            launch(sent_outer, lambda k=k: (block, block, in_send.at[0, k], in_recv.at[0, k], inner_peer))
-            launch(sent_outer, lambda k=k: (block, block, in_send.at[1, k], in_recv.at[2, k], across_inner))
-
-    for k in range(chunks):
-        forward(k)
-
-    row_at = lax.broadcasted_iota(jnp.int32, (rows, width), 0) + me * rows
-    col_at = lax.broadcasted_iota(jnp.int32, (rows, width), 1)
-    polar = math.pi * (row_at.astype(jnp.float32) + 0.5) / total_rows
-    azimuth = 2.0 * math.pi * col_at.astype(jnp.float32) / total_cols
-    sin_polar = jnp.sin(polar)
-    along_x = sin_polar * jnp.cos(azimuth)
-    along_y = sin_polar * jnp.sin(azimuth)
-    along_z = jnp.cos(polar)
-    for octant in range(4):
-        first, second = 1.0 - 2.0 * (octant % 2), 1.0 - 2.0 * (octant // 2)
-        argument = phase_scale * (first * along_x + second * along_y + along_z)
-        cosine[octant] = jnp.cos(argument)
-        sine[octant] = jnp.sin(argument)
+
+    def ring_copy(at):
+        exists, device, begin = rings[at]
+        return remote(
+            near.at[own_near], near.at[pl.ds(begin, 2 * children)], ring_send.at[at],
+            ring_recv.at[at], device,
+        )
+
+    for at in range(2):
+        pl.when(rings[at][0])(lambda: ring_copy(at).start())
+    pl.when(outer)(lambda: each(direct, chunks, lambda k: advance(k, outer_supply)))
+    for copy in (incoming_load, child_load, parent_load):
+        copy.start()
     for copy in table_loads:
         copy.wait()
-    loads[0].wait()
-    loads[1].wait()
+    theta_load.wait()
+    phi_load.wait()
     side_rows = aligned(total_rows // 2 * side, total_rows // 2)
     phi_t[...] = phi[...].T
     theta_t[...] = theta[side_rows].T
 
     def phases(child):
         octant = octant_s[child]
-        mirrored = octant // 4
+        mirrored = lax.shift_right_logical(octant, 2)
         held = octant + mirrored * (7 - 2 * octant)
         return held, (1 - 2 * mirrored).astype(jnp.float32)
 
+    def out_copy(k, at):
+        if at == 0:
+            begin, device = 2 * rows * (1 - side) + rows * (1 - x), partner
+        else:
+            begin, device = 2 * rows * side + rows * (at - 1), outer_peer[at - 1]
+        return remote(
+            spread.at[part(k), aligned(begin, rows)], rows_in.at[x, part(k)], out_send.at[0],
+            out_recv.at[k], device,
+        )
+
     def theta_stage(k):
-        own, near_z, far_z = 2 * depth * 3 * side, 2 * depth * (2 - side), 2 * depth * 3 * (1 - side)
-        for at, start in enumerate((own, near_z, far_z)):
-            landed(gathered.at[part(k), aligned(start, 2 * depth)], in_send.at[0, k], in_recv.at[at, k])
-        block = jnp.concatenate([gathered[k * group + j] for j in range(group)], axis=1)
+        if k < direct:
+            traded(k)
+        if direct <= k + early < chunks:
+            advance(k + early, inner_supply)
+        gathered[part(k), own_depth] = near[
+            pl.ds(2 * (children + starts[k]), 2 * sizes[k]), :, own_half
+        ]
+        landed(gathered.at[part(k), pl.ds(0, 6 * depth)], in_send.at[0], in_recv.at[k])
+        planes = range(2 * starts[k], 2 * (starts[k] + sizes[k]))
+        block = jnp.concatenate([gathered[j] for j in planes], axis=1)
         product = precise(theta[side_rows], block)
-        for j in range(group):
-            spread[k * group + j] = product[:, j * half : (j + 1) * half]
-        rows_in[x, part(k)] = spread[part(k), aligned(2 * rows * (1 - side) + rows * x, rows)]
-        launch(sent_inner, lambda k=k: (spread.at[part(k), aligned(2 * rows * (1 - side) + rows * (1 - x), rows)], rows_in.at[x, part(k)], out_send.at[0, k], out_recv.at[x, k], partner))
-        for at in range(2):
-            launch(sent_inner, lambda k=k, at=at: (spread.at[part(k), aligned(2 * rows * side + rows * at, rows)], rows_in.at[x, part(k)], out_send.at[1 + at, k], out_recv.at[x, k], outer_peer[at]))
+        for at, j in enumerate(planes):
+            spread[j] = product[:, at * half : (at + 1) * half]
+        for at in (1, 2, 0):
+            out_copy(k, at).start()
+        rows_in[x, part(k)] = spread[
+            part(k), aligned(2 * rows * (1 - side) + rows * x, rows)
+        ]
 
     windows = parent_windows(children, parents, 2, 6)
 
+    def parent_copy(at, p):
+        return remote(
+            wide.at[parents + p], wide.at[2 * parents * at + p], parent_send.at[at, p],
+            parent_recv.at[at, p], (upper, lower)[at],
+        )
+
     def shift_stage(k):
-        @pl.when(inner)
-        def _():
-            landed(rows_in.at[1 - x, part(k)], out_send.at[0, k], out_recv.at[1 - x, k])
-
-        @pl.when(outer)
-        def _():
-            for at in range(2):
-                landed(rows_in.at[at, part(k)], out_send.at[0, k], out_recv.at[at, k])
-
+        pl.when(inner)(
+            lambda: landed(rows_in.at[1 - x, part(k)], out_send.at[0], out_recv.at[k])
+        )
+        pl.when(outer)(lambda: landed(rows_in.at[:, part(k)], out_send.at[0], out_recv.at[k]))
         block = jnp.concatenate(
-            [rows_in[at, part(k)].reshape(group * rows, half) for at in range(2)], axis=1
+            [rows_in[at, part(k)].reshape(2 * sizes[k] * rows, half) for at in range(2)], axis=1
         )
         product = precise(block, phi[...])
-        for i in range(per_chunk):
-            child = k * per_chunk + i
-            held, sign = phases(child)
-            slot = parent_s[child] - box * parents
-            for t in range(0, rows, 8):
-                tile = slice(t, t + 8)
+        members = range(starts[k], starts[k] + sizes[k])
+        angles = [phases(child) for child in members]
+        slots = [parent_s[child] - box * parents for child in members]
+        belongs = [[(slot == p).astype(jnp.float32) for slot in slots] for p in range(parents)]
+        for t in range(0, rows, 8):
+            tile = slice(t, t + 8)
+            moved = []
+            for i, (held, sign) in enumerate(angles):
                 real = product[2 * i * rows + t : 2 * i * rows + t + 8]
                 imag = product[(2 * i + 1) * rows + t : (2 * i + 1) * rows + t + 8]
                 cos, sin = cosine[held, tile], sign * sine[held, tile]
-                moved = (cos * real - sin * imag, sin * real + cos * imag)
-                for p, (low, high) in enumerate(windows):
-                    if not low <= child < high:
+                moved.append((cos * real - sin * imag, sin * real + cos * imag))
+            for p, (low, high) in enumerate(windows):
+                for plane in range(2):
+                    terms = [
+                        belongs[p][i] * moved[i][plane]
+                        for i, child in enumerate(members) if low <= child < high
+                    ]
+                    if not terms:
                         continue
-                    belongs = (slot == p).astype(jnp.float32)
-                    for plane in range(2):
-                        term = belongs * moved[plane]
-                        if child == low:
-                            wide[parents + p, plane, tile] = term
-                        else:
-                            wide[parents + p, plane, tile] += term
+                    if low not in members:
+                        terms.insert(0, wide[parents + p, plane, tile])
+                    wide[parents + p, plane, tile] = functools.reduce(jnp.add, terms)
         for p, (low, high) in enumerate(windows):
-            if k * per_chunk < high <= (k + 1) * per_chunk:
-                for at, (exists, device) in enumerate(((has_upper, upper), (has_lower, lower))):
-                    @pl.when(exists)
-                    def _():
-                        remote(
-                            wide.at[parents + p], wide.at[2 * parents * at + p],
-                            parent_send.at[at, p], parent_recv.at[at, p], device,
-                        ).start()
-
-    for step in range(chunks + 1):
+            if high - 1 in members:
+                for at in range(2):
+                    pl.when(rings[at][0])(lambda: parent_copy(at, p).start())
+
+    shift_lag = 1
+
+    def up_step(step):
         if step < chunks:
-            pl.when(inner)(functools.partial(theta_stage, step))
-        if step >= 1:
-            shift_stage(step - 1)
-
-    loads[2].wait()
-    loads[4].wait()
+            pl.when(inner)(lambda: theta_stage(step))
+        if step >= shift_lag:
+            shift_stage(step - shift_lag)
+
+    each(0, chunks + shift_lag, up_step)
+
+    incoming_load.wait()
+    parent_load.wait()
     for at, exists in enumerate((has_lower, has_upper)):
         @pl.when(exists)
         def _():
             for p in range(parents):
                 landed(wide.at[2 * parents * at + p], parent_send.at[at, p], parent_recv.at[at, p])
 
-    tiles = rows // 8
-
-    def translate_tile(step, carry):
-        p, t = lax.div(step, tiles), lax.rem(step, tiles)
-        tile = pl.ds(pl.multiple_of(t * 8, 8), 8)
-        real, imag = local_ref[p, 0, tile], local_ref[p, 1, tile]
+    def translate_parent(p):
         length = parent_len_s[p]
+        entries = []
         for column in range(parent_src_s.shape[1]):
             at = within(parent_src_s[p, column] - (box - 1) * parents, 3 * parents)
-            op = parent_op_s[p, column]
-            live = (column < length).astype(jnp.float32)
-            op_real, op_imag = live * parent_ops[op, 0, tile], live * parent_ops[op, 1, tile]
-            re, im = wide[at, 0, tile], wide[at, 1, tile]
-            real = real + (op_real * re - op_imag * im)
-            imag = imag + (op_real * im + op_imag * re)
-        local_ref[p, 0, tile] = real
-        local_ref[p, 1, tile] = imag
+            entries.append((at, parent_op_s[p, column], (column < length).astype(jnp.float32)))
+        for t in range(0, rows, 8):
+            tile = slice(t, t + 8)
+            real, imag = local_ref[p, 0, tile], local_ref[p, 1, tile]
+            for at, op, live in entries:
+                op_real, op_imag = live * parent_ops[op, 0, tile], live * parent_ops[op, 1, tile]
+                re, im = wide[at, 0, tile], wide[at, 1, tile]
+                real = real + (op_real * re - op_imag * im)
+                imag = imag + (op_real * im + op_imag * re)
+            local_ref[p, 0, tile] = real
+            local_ref[p, 1, tile] = imag
+
+    def translate_step(p, carry):
+        translate_parent(p)
         return carry
 
-    lax.fori_loop(0, parents * tiles, translate_tile, 0)
+    lax.fori_loop(0, parents, translate_step, 0)
 
     z_local = z - 2 * side
     own_rows = aligned(2 * rows * z_local + rows * x, rows)
     partner_rows = aligned(2 * rows * z_local + rows * (1 - x), rows)
 
+    def back_copy(k):
+        return remote(
+            back.at[1 - x, part(k)], held_rows.at[part(k), own_rows], back_send.at[0],
+            back_recv.at[k], partner,
+        )
+
+    def raw_copy(k, relayed):
+        source, target, device = back.at[x, part(k)], held_rows.at[part(k), own_rows], inner_peer
+        if relayed and k < direct:
+            source, device = back.at[1 - x, part(k)], inner_diagonal
+        elif relayed:
+            source = target = held_rows.at[part(k), partner_rows]
+        return remote(source, target, raw_send.at[0], raw_recv.at[k], device)
+
     def unshift_stage(k):
         fields_in = []
-        for i in range(per_chunk):
-            child = k * per_chunk + i
+        for child in range(starts[k], starts[k] + sizes[k]):
             held, sign = phases(child)
             slot = within(parent_s[child] - box * parents, parents)
             cos, sin = cosine[held], sign * sine[held]
@@ -594,36 +669,66 @@
             fields_in += [cos * real + sin * imag, cos * imag - sin * real]
         product = precise(jnp.concatenate(fields_in, axis=0), phi_t[...])
         for at in range(2):
-            back[at, part(k)] = product[:, at * half : (at + 1) * half].reshape(group, rows, half)
-        held_rows[part(k), own_rows] = back[x, part(k)]
-        launch(sent, lambda k=k: (back.at[1 - x, part(k)], held_rows.at[part(k), own_rows], back_send.at[k], back_recv.at[k], partner))
+            back[at, part(k)] = product[:, at * half : (at + 1) * half].reshape(
+                2 * sizes[k], rows, half
+            )
+        if k >= direct:
+            back_copy(k).start()
+
+        @pl.when(inner)
+        def _():
+            if k < direct:
+                back_copy(k).start()
+            held_rows[part(k), own_rows] = back[x, part(k)]
+
+        @pl.when(outer)
+        def _():
+            raw_copy(k, 0).start()
+            if k < direct:
+                raw_copy(k, 1).start()
 
     def raise_stage(k):
-        landed(held_rows.at[part(k), partner_rows], back_send.at[k], back_recv.at[k])
-        launch(sent_outer, lambda k=k: (
-            held_rows.at[part(k), aligned(2 * rows * side, 2 * rows)],
-            held_rows.at[part(k), aligned(2 * rows * side, 2 * rows)],
-            raw_send.at[k], raw_recv.at[k], inner_peer,
-        ))
+        if k >= direct:
+            landed(held_rows.at[part(k), partner_rows], back_send.at[0], back_recv.at[k])
+            raw_copy(k, 1).start()
+
+    def swap_copy(k):
+        return remote(
+            partial.at[part(k), aligned(4 * depth * (1 - side), 4 * depth)], other.at[part(k)],
+            swap_send.at[0], swap_recv.at[k], across_inner,
+        )
 
     def gather_stage(k):
-        landed(held_rows.at[part(k), partner_rows], back_send.at[k], back_recv.at[k])
+        landed(held_rows.at[part(k), partner_rows], back_send.at[0], back_recv.at[k])
         landed(
-            held_rows.at[part(k), aligned(2 * rows * side, 2 * rows)], raw_send.at[k], raw_recv.at[k]
-        )
-        block = jnp.concatenate([held_rows[k * group + j] for j in range(group)], axis=1)
+            held_rows.at[part(k), aligned(2 * rows * side, 2 * rows)], raw_send.at[0],
+            raw_recv.at[k],
+        )
+        planes = range(2 * starts[k], 2 * (starts[k] + sizes[k]))
+        block = jnp.concatenate([held_rows[j] for j in planes], axis=1)
         product = precise(theta_t[...], block)
-        for j in range(group):
-            partial[k * group + j] = product[:, j * half : (j + 1) * half]
-        launch(sent_inner, lambda k=k: (partial.at[part(k), aligned(4 * depth * (1 - side), 4 * depth)], other.at[part(k)], swap_send.at[k], swap_recv.at[k], across_inner))
+        for at, j in enumerate(planes):
+            partial[j] = product[:, at * half : (at + 1) * half]
+        swap_copy(k).start()
+
+    def final_copy(k, at):
+        if at == 0:
+            begin, device = 2 * depth * (1 - side) + depth * (1 - x), partner
+        else:
+            begin, device = 2 * depth * side + depth * (at - 1), outer_peer[at - 1]
+        return remote(
+            total.at[part(k), aligned(begin, depth)], final.at[x, part(k)], final_send.at[0],
+            final_recv.at[k], device,
+        )
 
     def combine_stage(k):
-        landed(other.at[part(k)], swap_send.at[k], swap_recv.at[k])
+        landed(other.at[part(k)], swap_send.at[0], swap_recv.at[k])
         total[part(k)] = partial[part(k), aligned(4 * depth * side, 4 * depth)] + other[part(k)]
-        final[x, part(k)] = total[part(k), aligned(2 * depth * (1 - side) + depth * x, depth)]
-        launch(sent_inner, lambda k=k: (total.at[part(k), aligned(2 * depth * (1 - side) + depth * (1 - x), depth)], final.at[x, part(k)], final_send.at[0, k], final_recv.at[x, k], partner))
-        for at in range(2):
-            launch(sent_inner, lambda k=k, at=at: (total.at[part(k), aligned(2 * depth * side + depth * at, depth)], final.at[x, part(k)], final_send.at[1 + at, k], final_recv.at[x, k], outer_peer[at]))
+        for at in (1, 2, 0):
+            final_copy(k, at).start()
+        final[x, part(k)] = total[
+            part(k), aligned(2 * depth * (1 - side) + depth * x, depth)
+        ]
 
     def child_translate(child, carry):
         real = jnp.zeros((depth, out_ref.shape[2]), jnp.float32)
@@ -642,66 +747,68 @@
         return carry
 
     def finish_stage(k):
-        @pl.when(inner)
-        def _():
-            landed(final.at[1 - x, part(k)], final_send.at[0, k], final_recv.at[1 - x, k])
-
-        @pl.when(outer)
-        def _():
-            for at in range(2):
-                landed(final.at[at, part(k)], final_send.at[0, k], final_recv.at[at, k])
-
+        pl.when(inner)(
+            lambda: landed(final.at[1 - x, part(k)], final_send.at[0], final_recv.at[k])
+        )
+        pl.when(outer)(lambda: landed(final.at[:, part(k)], final_send.at[0], final_recv.at[k]))
         for at in range(2):
             columns = slice(at * half, (at + 1) * half)
             out_ref[part(k), :, columns] += final[at, part(k)]
 
-    lag = 2
-    for step in range(chunks + lag + 1):
+    child_load.wait()
+    for at, (exists, start) in enumerate(((has_lower, 0), (has_upper, 4 * children))):
+        @pl.when(exists)
+        def _():
+            landed(near.at[pl.ds(start, 2 * children)], ring_send.at[at], ring_recv.at[at])
+
+    lag, wait_lag, end_lag = 3, 2, 2
+
+    def down_step(step):
         if step < chunks:
             unshift_stage(step)
         if 1 <= step <= chunks:
-            pl.when(outer)(functools.partial(raise_stage, step - 1))
-        if step == lag:
-            loads[3].wait()
-            loads[5].wait()
-            for at, (exists, start) in enumerate(((has_lower, 0), (has_upper, 4 * children))):
-                @pl.when(exists)
-                def _():
-                    landed(near.at[pl.ds(start, 2 * children)], ring_send.at[at], ring_recv.at[at])
-            parent_rad_ref[...] = wide[parents : 2 * parents]
+            pl.when(outer)(lambda: raise_stage(step - 1))
         if lag <= step < chunks + lag:
-            first = (step - lag) * per_chunk
-            lax.fori_loop(first, first + per_chunk, child_translate, 0)
-            pl.when(inner)(functools.partial(gather_stage, step - lag))
-        if lag + 1 <= step:
-            pl.when(inner)(functools.partial(combine_stage, step - lag - 1))
-    for k in range(chunks):
-        finish_stage(k)
-
-    for build in sent:
-        remote(*build()).wait_send()
-
-    @pl.when(inner)
-    def _():
-        for build in sent_inner:
-            remote(*build()).wait_send()
-
-    @pl.when(outer)
-    def _():
-        for build in sent_outer:
-            remote(*build()).wait_send()
-
+            pl.when(inner)(lambda: gather_stage(step - lag))
+            first = starts[step - lag]
+            lax.fori_loop(first, first + sizes[step - lag], child_translate, 0)
+        if step >= lag + wait_lag:
+            pl.when(inner)(lambda: combine_stage(step - lag - wait_lag))
+        if step >= lag + wait_lag + end_lag:
+            finish_stage(step - lag - wait_lag - end_lag)
+
+    each(0, chunks + lag + wait_lag, down_step)
+    parent_rad_ref[...] = wide[parents : 2 * parents]
+    each(chunks - end_lag, chunks, finish_stage)
+
+    def settled(target, send):
+        remote(target, target, send, final_recv.at[0], partner).wait_send()
+
+    everything = pl.ds(0, 2 * children)
+    later = pl.ds(2 * starts[direct], 2 * (children - starts[direct]))
+
+    def settle_inner():
+        settled(gathered.at[everything, pl.ds(0, depth)], pre_send.at[0])
+        settled(gathered.at[everything, pl.ds(0, 2 * depth)], in_send.at[0])
+        settled(spread.at[everything, pl.ds(0, 3 * rows)], out_send.at[0])
+        settled(held_rows.at[everything, pl.ds(0, rows)], back_send.at[0])
+        settled(partial.at[everything, pl.ds(0, 4 * depth)], swap_send.at[0])
+        settled(total.at[everything, pl.ds(0, 3 * depth)], final_send.at[0])
+
+    def settle_outer():
+        settled(gathered.at[later, pl.ds(0, depth)], pre_send.at[0])
+        settled(gathered.at[everything, pl.ds(0, 4 * depth)], in_send.at[0])
+        settled(held_rows.at[later, pl.ds(0, rows)], back_send.at[0])
+        settled(held_rows.at[everything, pl.ds(0, 2 * rows)], raw_send.at[0])
+
+    pl.when(inner)(settle_inner)
+    pl.when(outer)(settle_outer)
     for at, (exists, device, start) in enumerate(rings):
         @pl.when(exists)
         def _():
-            remote(
-                rad_h, near.at[pl.ds(start, 2 * children)], ring_send.at[at], ring_recv.at[at], device
-            ).wait_send()
+            ring_copy(at).wait_send()
             for p in range(parents):
-                remote(
-                    wide.at[parents + p], wide.at[2 * parents * at + p],
-                    parent_send.at[at, p], parent_recv.at[at, p], device,
-                ).wait_send()
+                parent_copy(at, p).wait_send()
 
 
 def deliver_body(*refs):
@@ -734,8 +841,8 @@
     children, _, depth, phi_child = child_rad.shape
     parents, _, rows, width = parent_incoming.shape
     total_rows, total_depth = theta_interp.shape
-    per_chunk = 2
-    chunks = children // per_chunk
+    sizes = (2,) * (children // 2)
+    chunks = len(sizes)
     half = phi_child // 2
     planes = 2 * children
     vmem = pl.BlockSpec(memory_space=pltpu.VMEM)
@@ -767,32 +874,31 @@
         room(2, planes, depth, half),
         *(pltpu.SMEM(table.shape, jnp.int32) for table in tables),
         dma((14,)),
+        dma((1,)),
         dma((chunks,)),
+        dma((1,)),
         dma((chunks,)),
+        dma((1,)),
         dma((chunks,)),
-        dma((2, chunks)),
-        dma((3, chunks)),
-        dma((3, chunks)),
-        dma((2, chunks)),
         dma((2,)),
         dma((2,)),
         dma((2, parents)),
         dma((2, parents)),
+        dma((1,)),
         dma((chunks,)),
+        dma((1,)),
         dma((chunks,)),
+        dma((1,)),
         dma((chunks,)),
+        dma((1,)),
         dma((chunks,)),
-        dma((chunks,)),
-        dma((chunks,)),
-        dma((3, chunks)),
-        dma((2, chunks)),
     ]
     operands = (
         *tables, child_rad.reshape(planes, depth, phi_child), parent_incoming, theta_interp,
         phi_interp, child_ops, parent_ops,
     )
     anterp, local, rad = pl.pallas_call(
-        functools.partial(fused_body, lax.axis_size("box"), per_chunk),
+        functools.partial(fused_body, lax.axis_size("box"), sizes),
         out_shape=(
             jax.ShapeDtypeStruct((planes, depth, phi_child), jnp.float32),
             jax.ShapeDtypeStruct(parent_incoming.shape, jnp.float32),
@@ -830,7 +936,7 @@
     parent_count, _, theta_parent, phi_parent = parent_incoming.shape
     theta_total = theta_interp.shape[0]
     dir_count = lax.axis_size("dir")
-    if dir_count == 8 and theta_child % 8 == 0 and phi_child % 256 == 0 and child_count % 2 == 0:
+    if dir_count == 8 and theta_child % 8 == 0 and phi_child % 256 == 0 and child_count % 2 == 0 and child_count >= 8:
         return fused(
             child_rad, parent_incoming, theta_interp, phi_interp, child_ops, parent_ops, child_parent,
             child_octant, far_child_src, far_child_op, far_child_len, far_parent_src, far_parent_op,

time: 80.3 us -> 75 us (0.934)
  Pallas kernels: 79.2 us -> 74.2 us
    pallas_call x1, Pallas kernels: 78 us -> 73.1 us  [fused(): pl.pallas_call(functools.partial(fused_body, lax.axis_size('box'), sizes)...]
where the time goes in v2:
time: 75 us; the launch traced here: 74.9 us
  Pallas kernels  74.2 us (99%)
    pallas_call x1, Pallas kernels, fused(): pl.pallas_call(functools.partial(fused_body, lax.axis_size('box'), sizes)...  73.1 us

profile of v2, /device:TPU:4, one launch (start us, length us, event | category | flops | bytes accessed | tf_op | source)
XLA Modules:
  0.0 74.9 jit_solution(8555825983114361826)
XLA Ops:
  0.6 73.1 %level_pass.1 = (f32[32,16,256]{2,1,0:T(8,128)S(1)}, f32[4,2,32,512]{3,2,1,0:T(8,128)S(1)}, f32[4,2,32,512]{3,2,1,0:T(8,128)S(1)}) custom-call(s32[16]{0:T(128)} %refs_0_.1, s32[16]{0:T(128)} %refs_1_.1, s32[16,16]{1,0:T(8,128)} %refs_2_.1, s32[16,16]{1,0:T(8,128)} %refs_3_.1, s32[16]{0:T(128)} %refs_4_.1, s32[4,8]{1,0:T(4,128)} %refs_5_.1, s32[4,8]{1,0:T(4,128)} %refs_6_.1, ...), custom_call_target="tpu_custom_call" | custom-call | tf_op jit(solution)/shard_map/level_pass/pallas_call | solution.py:900
  73.7 1.2 %deliver.1 = (f32[32,16,256]{2,1,0:T(8,128)}, f32[4,2,32,512]{3,2,1,0:T(8,128)}, f32[4,2,32,512]{3,2,1,0:T(8,128)}) custom-call(f32[32,16,256]{2,1,0:T(8,128)S(1)} %get-tuple-element.9.refs_0_, f32[4,2,32,512]{3,2,1,0:T(8,128)S(1)} %get-tuple-element.10.refs_1_, f32[4,2,32,512]{3,2,1,0:T(8,128)S(1)} %get-tuple-element.11.refs_2_), custom_call_target="tpu_custom_call" | custom-call | tf_op jit(solution)/shard_map/deliver/pallas_call | solution.py:827

commit v3 on v2

--- a/solution.py
+++ b/solution.py
@@ -635,11 +635,6 @@
             local_ref[p, 0, tile] = real
             local_ref[p, 1, tile] = imag
 
-    def translate_step(p, carry):
-        translate_parent(p)
-        return carry
-
-    lax.fori_loop(0, parents, translate_step, 0)
 
     z_local = z - 2 * side
     own_rows = aligned(2 * rows * z_local + rows * x, rows)
@@ -761,15 +756,21 @@
         def _():
             landed(near.at[pl.ds(start, 2 * children)], ring_send.at[at], ring_recv.at[at])
 
-    lag, wait_lag, end_lag = 3, 2, 2
+    lag, wait_lag, end_lag = 2, 2, 2
 
     def down_step(step):
         if step < chunks:
+            reached = starts[step] + sizes[step]
+            for p, (low, high) in enumerate(windows):
+                if starts[step] <= low < reached:
+                    translate_parent(p)
             unshift_stage(step)
         if 1 <= step <= chunks:
             pl.when(outer)(lambda: raise_stage(step - 1))
         if lag <= step < chunks + lag:
             pl.when(inner)(lambda: gather_stage(step - lag))
+            if step == lag:
+                parent_rad_ref[...] = wide[parents : 2 * parents]
             first = starts[step - lag]
             lax.fori_loop(first, first + sizes[step - lag], child_translate, 0)
         if step >= lag + wait_lag:
@@ -778,7 +779,6 @@
             finish_stage(step - lag - wait_lag - end_lag)
 
     each(0, chunks + lag + wait_lag, down_step)
-    parent_rad_ref[...] = wide[parents : 2 * parents]
     each(chunks - end_lag, chunks, finish_stage)
 
     def settled(target, send):
@@ -841,7 +841,7 @@
     children, _, depth, phi_child = child_rad.shape
     parents, _, rows, width = parent_incoming.shape
     total_rows, total_depth = theta_interp.shape
-    sizes = (2,) * (children // 2)
+    sizes = (2,) * (children // 2 - 1) + (1, 1)
     chunks = len(sizes)
     half = phi_child // 2
     planes = 2 * children

time: 75 us -> 74.3 us (level)
  no operation moved by 1% of the time
where the time goes in v3:
time: 74.3 us; the launch traced here: 74.2 us
  Pallas kernels  73.5 us (99%)
    pallas_call x1, Pallas kernels, fused(): pl.pallas_call(functools.partial(fused_body, lax.axis_size('box'), sizes)...  72.3 us

profile of v3, /device:TPU:4, one launch (start us, length us, event | category | flops | bytes accessed | tf_op | source)
XLA Modules:
  0.0 74.2 jit_solution(15943859284454580855)
XLA Ops:
  0.6 72.3 %level_pass.1 = (f32[32,16,256]{2,1,0:T(8,128)S(1)}, f32[4,2,32,512]{3,2,1,0:T(8,128)S(1)}, f32[4,2,32,512]{3,2,1,0:T(8,128)S(1)}) custom-call(s32[16]{0:T(128)} %refs_0_.1, s32[16]{0:T(128)} %refs_1_.1, s32[16,16]{1,0:T(8,128)} %refs_2_.1, s32[16,16]{1,0:T(8,128)} %refs_3_.1, s32[16]{0:T(128)} %refs_4_.1, s32[4,8]{1,0:T(4,128)} %refs_5_.1, s32[4,8]{1,0:T(4,128)} %refs_6_.1, ...), custom_call_target="tpu_custom_call" | custom-call | tf_op jit(solution)/shard_map/level_pass/pallas_call | solution.py:900
  73.0 1.2 %deliver.1 = (f32[32,16,256]{2,1,0:T(8,128)}, f32[4,2,32,512]{3,2,1,0:T(8,128)}, f32[4,2,32,512]{3,2,1,0:T(8,128)}) custom-call(f32[32,16,256]{2,1,0:T(8,128)S(1)} %get-tuple-element.9.refs_0_, f32[4,2,32,512]{3,2,1,0:T(8,128)S(1)} %get-tuple-element.10.refs_1_, f32[4,2,32,512]{3,2,1,0:T(8,128)S(1)} %get-tuple-element.11.refs_2_), custom_call_target="tpu_custom_call" | custom-call | tf_op jit(solution)/shard_map/deliver/pallas_call | solution.py:827

commit v4 on v3

--- a/solution.py
+++ b/solution.py
@@ -356,6 +356,8 @@
 
     partner = at_place(2 * z + 1 - x)
     outer_peer = [at_place(6 * side + at) for at in range(2)]
+    far_first = (1 - x, x)
+    outer_far_first = [at_place(6 * side + at) for at in far_first]
     inner_peers = [at_place(2 * (1 + side) + at) for at in range(2)]
     inner_peer = at_place(2 * (1 + side) + x)
     across_inner = at_place(2 * (2 - side) + x)
@@ -468,8 +470,8 @@
 
     def outer_supply(k, relayed):
         return [
+            supply(k, relayed, (across_inner, across_diagonal)),
             supply(k, relayed, (inner_peer, inner_diagonal)),
-            supply(k, relayed, (across_inner, across_diagonal)),
         ]
 
     def start(copies):
@@ -529,7 +531,7 @@
         if at == 0:
             begin, device = 2 * rows * (1 - side) + rows * (1 - x), partner
         else:
-            begin, device = 2 * rows * side + rows * (at - 1), outer_peer[at - 1]
+            begin, device = 2 * rows * side + rows * far_first[at - 1], outer_far_first[at - 1]
         return remote(
             spread.at[part(k), aligned(begin, rows)], rows_in.at[x, part(k)], out_send.at[0],
             out_recv.at[k], device,
@@ -538,8 +540,6 @@
     def theta_stage(k):
         if k < direct:
             traded(k)
-        if direct <= k + early < chunks:
-            advance(k + early, inner_supply)
         gathered[part(k), own_depth] = near[
             pl.ds(2 * (children + starts[k]), 2 * sizes[k]), :, own_half
         ]
@@ -551,6 +551,8 @@
             spread[j] = product[:, at * half : (at + 1) * half]
         for at in (1, 2, 0):
             out_copy(k, at).start()
+        if direct <= k + early < chunks:
+            advance(k + early, inner_supply)
         rows_in[x, part(k)] = spread[
             part(k), aligned(2 * rows * (1 - side) + rows * x, rows)
         ]
@@ -710,7 +712,7 @@
         if at == 0:
             begin, device = 2 * depth * (1 - side) + depth * (1 - x), partner
         else:
-            begin, device = 2 * depth * side + depth * (at - 1), outer_peer[at - 1]
+            begin, device = 2 * depth * side + depth * far_first[at - 1], outer_far_first[at - 1]
         return remote(
             total.at[part(k), aligned(begin, depth)], final.at[x, part(k)], final_send.at[0],
             final_recv.at[k], device,
@@ -758,6 +760,40 @@
 
     lag, wait_lag, end_lag = 2, 2, 2
 
+    def settled(target, send):
+        remote(target, target, send, final_recv.at[0], partner).wait_send()
+
+    everything = pl.ds(0, 2 * children)
+    later = pl.ds(2 * starts[direct], 2 * (children - starts[direct]))
+
+    def settle_up_inner():
+        settled(gathered.at[everything, pl.ds(0, depth)], pre_send.at[0])
+        settled(gathered.at[everything, pl.ds(0, 2 * depth)], in_send.at[0])
+        settled(spread.at[everything, pl.ds(0, 3 * rows)], out_send.at[0])
+
+    def settle_up_outer():
+        settled(gathered.at[later, pl.ds(0, depth)], pre_send.at[0])
+        settled(gathered.at[everything, pl.ds(0, 4 * depth)], in_send.at[0])
+
+    def settle_up():
+        pl.when(inner)(settle_up_inner)
+        pl.when(outer)(settle_up_outer)
+        for at, (exists, device, begin) in enumerate(rings):
+            @pl.when(exists)
+            def _():
+                ring_copy(at).wait_send()
+                for p in range(parents):
+                    parent_copy(at, p).wait_send()
+
+    def settle_inner():
+        settled(held_rows.at[everything, pl.ds(0, rows)], back_send.at[0])
+        settled(partial.at[everything, pl.ds(0, 4 * depth)], swap_send.at[0])
+        settled(total.at[everything, pl.ds(0, 3 * depth)], final_send.at[0])
+
+    def settle_outer():
+        settled(held_rows.at[later, pl.ds(0, rows)], back_send.at[0])
+        settled(held_rows.at[everything, pl.ds(0, 2 * rows)], raw_send.at[0])
+
     def down_step(step):
         if step < chunks:
             reached = starts[step] + sizes[step]
@@ -771,6 +807,7 @@
             pl.when(inner)(lambda: gather_stage(step - lag))
             if step == lag:
                 parent_rad_ref[...] = wide[parents : 2 * parents]
+                settle_up()
             first = starts[step - lag]
             lax.fori_loop(first, first + sizes[step - lag], child_translate, 0)
         if step >= lag + wait_lag:
@@ -780,35 +817,8 @@
 
     each(0, chunks + lag + wait_lag, down_step)
     each(chunks - end_lag, chunks, finish_stage)
-
-    def settled(target, send):
-        remote(target, target, send, final_recv.at[0], partner).wait_send()
-
-    everything = pl.ds(0, 2 * children)
-    later = pl.ds(2 * starts[direct], 2 * (children - starts[direct]))
-
-    def settle_inner():
-        settled(gathered.at[everything, pl.ds(0, depth)], pre_send.at[0])
-        settled(gathered.at[everything, pl.ds(0, 2 * depth)], in_send.at[0])
-        settled(spread.at[everything, pl.ds(0, 3 * rows)], out_send.at[0])
-        settled(held_rows.at[everything, pl.ds(0, rows)], back_send.at[0])
-        settled(partial.at[everything, pl.ds(0, 4 * depth)], swap_send.at[0])
-        settled(total.at[everything, pl.ds(0, 3 * depth)], final_send.at[0])
-
-    def settle_outer():
-        settled(gathered.at[later, pl.ds(0, depth)], pre_send.at[0])
-        settled(gathered.at[everything, pl.ds(0, 4 * depth)], in_send.at[0])
-        settled(held_rows.at[later, pl.ds(0, rows)], back_send.at[0])
-        settled(held_rows.at[everything, pl.ds(0, 2 * rows)], raw_send.at[0])
-
     pl.when(inner)(settle_inner)
     pl.when(outer)(settle_outer)
-    for at, (exists, device, start) in enumerate(rings):
-        @pl.when(exists)
-        def _():
-            ring_copy(at).wait_send()
-            for p in range(parents):
-                parent_copy(at, p).wait_send()
 
 
 def deliver_body(*refs):

time: 74.3 us -> 73.6 us (level)
  no operation moved by 1% of the time
where the time goes in v4:
time: 73.6 us; the launch traced here: 73.5 us
  Pallas kernels  72.9 us (99%)
    pallas_call x1, Pallas kernels, fused(): pl.pallas_call(functools.partial(fused_body, lax.axis_size('box'), sizes)...  71.7 us

profile of v4, /device:TPU:4, one launch (start us, length us, event | category | flops | bytes accessed | tf_op | source)
XLA Modules:
  0.0 73.5 jit_solution(12301407536147697957)
XLA Ops:
  0.6 71.7 %level_pass.1 = (f32[32,16,256]{2,1,0:T(8,128)S(1)}, f32[4,2,32,512]{3,2,1,0:T(8,128)S(1)}, f32[4,2,32,512]{3,2,1,0:T(8,128)S(1)}) custom-call(s32[16]{0:T(128)} %refs_0_.1, s32[16]{0:T(128)} %refs_1_.1, s32[16,16]{1,0:T(8,128)} %refs_2_.1, s32[16,16]{1,0:T(8,128)} %refs_3_.1, s32[16]{0:T(128)} %refs_4_.1, s32[4,8]{1,0:T(4,128)} %refs_5_.1, s32[4,8]{1,0:T(4,128)} %refs_6_.1, ...), custom_call_target="tpu_custom_call" | custom-call | tf_op jit(solution)/shard_map/level_pass/pallas_call | solution.py:910
  72.3 1.2 %deliver.1 = (f32[32,16,256]{2,1,0:T(8,128)}, f32[4,2,32,512]{3,2,1,0:T(8,128)}, f32[4,2,32,512]{3,2,1,0:T(8,128)}) custom-call(f32[32,16,256]{2,1,0:T(8,128)S(1)} %get-tuple-element.9.refs_0_, f32[4,2,32,512]{3,2,1,0:T(8,128)S(1)} %get-tuple-element.10.refs_1_, f32[4,2,32,512]{3,2,1,0:T(8,128)S(1)} %get-tuple-element.11.refs_2_), custom_call_target="tpu_custom_call" | custom-call | tf_op jit(solution)/shard_map/deliver/pallas_call | solution.py:837

commit v5 on v4

--- a/solution.py
+++ b/solution.py
@@ -489,12 +489,18 @@
             start(copies(k + early, 0))
 
     def open_supply(copies):
-        for k in range(direct):
+        for k in range(1, direct):
             start(copies(k, 0))
             start(copies(k, 1))
         for k in range(direct, direct + early):
             start(copies(k, 0))
 
+    def open_first(copies):
+        start(copies(0, 0))
+        start(copies(0, 1))
+
+    pl.when(inner)(lambda: open_first(inner_supply))
+    pl.when(outer)(lambda: open_first(outer_supply))
     pl.when(inner)(lambda: start([trade(k) for k in range(direct)]))
     start([trade(k) for k in range(direct, direct + early)])
     pl.when(inner)(lambda: open_supply(inner_supply))

time: 73.6 us -> 73.7 us (level)
  no operation moved by 1% of the time
where the time goes in v5:
time: 73.7 us; the launch traced here: 73.5 us
  Pallas kernels  72.9 us (99%)
    pallas_call x1, Pallas kernels, fused(): pl.pallas_call(functools.partial(fused_body, lax.axis_size('box'), sizes)...  71.7 us

profile of v5, /device:TPU:4, one launch (start us, length us, event | category | flops | bytes accessed | tf_op | source)
XLA Modules:
  0.0 73.5 jit_solution(1133499293746577915)
XLA Ops:
  0.6 71.7 %level_pass.1 = (f32[32,16,256]{2,1,0:T(8,128)S(1)}, f32[4,2,32,512]{3,2,1,0:T(8,128)S(1)}, f32[4,2,32,512]{3,2,1,0:T(8,128)S(1)}) custom-call(s32[16]{0:T(128)} %refs_0_.1, s32[16]{0:T(128)} %refs_1_.1, s32[16,16]{1,0:T(8,128)} %refs_2_.1, s32[16,16]{1,0:T(8,128)} %refs_3_.1, s32[16]{0:T(128)} %refs_4_.1, s32[4,8]{1,0:T(4,128)} %refs_5_.1, s32[4,8]{1,0:T(4,128)} %refs_6_.1, ...), custom_call_target="tpu_custom_call" | custom-call | tf_op jit(solution)/shard_map/level_pass/pallas_call | solution.py:916
  72.3 1.2 %deliver.1 = (f32[32,16,256]{2,1,0:T(8,128)}, f32[4,2,32,512]{3,2,1,0:T(8,128)}, f32[4,2,32,512]{3,2,1,0:T(8,128)}) custom-call(f32[32,16,256]{2,1,0:T(8,128)S(1)} %get-tuple-element.9.refs_0_, f32[4,2,32,512]{3,2,1,0:T(8,128)S(1)} %get-tuple-element.10.refs_1_, f32[4,2,32,512]{3,2,1,0:T(8,128)S(1)} %get-tuple-element.11.refs_2_), custom_call_target="tpu_custom_call" | custom-call | tf_op jit(solution)/shard_map/deliver/pallas_call | solution.py:843
